TPU v7x, 32 devices: a whole 2x2x4 slice. The times are simulated.
32 devices in a mesh: stream: 4 (over x, core), tm: 8 (over z, y).
Axes of the slice: x: 2, y: 2, z: 4, core: 2. Of those that a mesh axis runs over, the one named last changes fastest.
Arguments:
- frames_in: bfloat16 [8, 3072, 1024], P('stream', 'tm'), may hold values from -45 to 45
- w_qkv: bfloat16 [1024, 3072], replicated, may hold values from -1 to 1
- grad_out: bfloat16 [8, 3072, 1024], P('stream', 'tm'), may hold values from -6 to 6
Outputs:
- grad_in: bfloat16 [8, 3072, 1024], P('stream', 'tm')
- grad_w: float32 [1024, 3072], P(('stream', 'tm'))
All inputs are finite; a program needn't handle non-finite values.
Results may differ from a plain program's by a relative error of at most 0.015.
Values may be sent and summed in bfloat16 or wider, within the bound.
A program may use at most 192 MiB of HBM per device.

v0:
```python
import jax
import jax.numpy as jnp
from jax import lax
from jax.sharding import PartitionSpec as P

HEADS = 8


def passed_along(value, axis, steps):
    count = lax.axis_size(axis)
    first, last = (max(0, -steps), min(count, count - steps))
    return lax.ppermute(value, axis, [(source, source + steps) for source in range(first, last)])


def local(frames_in, w_qkv, grad_out):
    records, frame_count, model_width = frames_in.shape
    head_size = model_width // HEADS
    score_scale = head_size ** (-0.5)
    flat_frames = frames_in.reshape(records * frame_count, model_width)
    qkv = jnp.dot(flat_frames, w_qkv, preferred_element_type=jnp.float32).astype(jnp.bfloat16)
    qkv = qkv.reshape(records, frame_count, 3 * model_width)
    key_value = qkv[..., model_width:]
    time_index = lax.axis_index("tm")
    previous = passed_along(key_value, "tm", 1)
    kv_all = jnp.concatenate([previous, key_value], 1)
    query_heads = qkv[..., :model_width].reshape(records, frame_count, HEADS, head_size)
    key_heads = kv_all[..., :model_width].reshape(records, 2 * frame_count, HEADS, head_size)
    value_heads = kv_all[..., model_width:].reshape(records, 2 * frame_count, HEADS, head_size)
    scores = (
        jnp.einsum("rfhd,rghd->rhfg", query_heads, key_heads, preferred_element_type=jnp.float32)
        * score_scale
    )
    columns = jnp.arange(2 * frame_count)
    valid = jnp.logical_or(columns >= frame_count, time_index > 0)
    scores = jnp.where(valid, scores, -1e30)
    peak = jnp.max(scores, axis=-1, keepdims=True)
    expo = jnp.exp(scores - peak)
    prob = expo / jnp.sum(expo, axis=-1, keepdims=True)
    prob_b = prob.astype(jnp.bfloat16)
    grad_heads = grad_out.reshape(records, frame_count, HEADS, head_size)
    dprob = jnp.einsum(
        "rfhd,rghd->rhfg", grad_heads, value_heads, preferred_element_type=jnp.float32
    )
    delta = jnp.sum(prob * dprob, axis=-1, keepdims=True)
    dscore = (prob * (dprob - delta) * score_scale).astype(jnp.bfloat16)
    grad_query = jnp.einsum(
        "rhfg,rghd->rfhd", dscore, key_heads, preferred_element_type=jnp.float32
    ).astype(jnp.bfloat16)
    grad_key = jnp.einsum(
        "rhfg,rfhd->rghd", dscore, query_heads, preferred_element_type=jnp.float32
    )
    grad_value = jnp.einsum(
        "rhfg,rfhd->rghd", prob_b, grad_heads, preferred_element_type=jnp.float32
    )
    grad_kv = jnp.concatenate(
        [
            grad_key.reshape(records, 2 * frame_count, model_width),
            grad_value.reshape(records, 2 * frame_count, model_width),
        ],
        -1,
    )
    earlier = grad_kv[:, :frame_count]
    own_part = grad_kv[:, frame_count:]
    returned = passed_along(earlier.astype(jnp.bfloat16), "tm", -1).astype(earlier.dtype)
    summed = (own_part + returned).astype(jnp.bfloat16)
    grad_cat = jnp.concatenate([grad_query.reshape(records, frame_count, model_width), summed], -1)
    grad_cat = grad_cat.reshape(records * frame_count, 3 * model_width)
    grad_frames = lax.dot_general(
        grad_cat, w_qkv, (((1,), (1,)), ((), ())), preferred_element_type=jnp.float32
    )
    grad_in = grad_frames.astype(jnp.bfloat16).reshape(records, frame_count, model_width)
    total_frames = records * frame_count * lax.axis_size("stream") * lax.axis_size("tm")
    full_terms = lax.dot_general(
        flat_frames, grad_cat, (((0,), (0,)), ((), ())), preferred_element_type=jnp.float32
    )
    partial_rows = lax.psum_scatter(
        full_terms.astype(jnp.bfloat16), "stream", scatter_dimension=0, tiled=True
    )
    reduced = lax.psum_scatter(partial_rows, "tm", scatter_dimension=0, tiled=True).astype(
        jnp.float32
    )
    grad_w = reduced * float(total_frames) ** (-0.5)
    return (grad_in, grad_w)


def solution(mesh):
    return jax.shard_map(
        local,
        mesh=mesh,
        in_specs=(P("stream", "tm", None), P(), P("stream", "tm", None)),
        out_specs=(P("stream", "tm", None), P(("stream", "tm"), None)),
        check_vma=False,
    )
```

profile of v0, /device:TPU:0, one launch (start us, length us, event | category | flops | bytes accessed | tf_op | source)
XLA Modules:
  0.0 410.3 jit_solution(16062657690577796575)
XLA Ops:
  7.2 0.0 copy-start
  7.2 0.0 reduce-scatter.5.cloned.1.call-start
  7.2 1.4 copy-done
  8.6 8.0 %convolution_convert_fusion = bf16[768,3072]{1,0:T(8,128)(2,1)S(1)} fusion(bf16[768,1024]{1,0:T(8,128)(2,1)S(1)} %bitcast.68, bf16[1024,3072]{1,0:T(8,128)(2,1)} %param.4), kind=kOutput, calls=%fused_computation.29 | convolution fusion | flops 4834197504 | bytes 12582912 | tf_op jit(solution)/shard_map/dot_general | solution.py:20
  16.6 0.0 copy-start.2
  16.6 2.1 copy-done.2
  18.7 2.1 slice.25
  20.8 4.6 %copy.39 = bf16[2,384,2048]{1,2,0:T(8,128)(2,1)} copy(bf16[2,384,2048]{2,1,0:T(8,128)(2,1)} %slice.25) | data formatting | bytes 6291456
  25.4 6.6 %collective-permute-start = (bf16[2,384,2048]{1,2,0:T(8,128)(2,1)}, bf16[2,384,2048]{1,2,0:T(8,128)(2,1)}, u32[]{:S(2)}, u32[]{:S(2)}) collective-permute-start(bf16[2,384,2048]{1,2,0:T(8,128)(2,1)} %copy.39), channel_id=1, source_target_pairs={{0,1},{1,2},{2,3},{3,4},{4,5},{5,6},{6,7},{8,9},{9,10},{10,11},{11... | collective-permute-start | bytes 9437192 | tf_op jit(solution)/shard_map/ppermute | solution.py:12
  32.1 2.7 slice.28
  34.7 1.9 copy.41
  36.6 2.6 copy.40
  39.2 58.7 %collective-permute-done = bf16[2,384,2048]{1,2,0:T(8,128)(2,1)} collective-permute-done((bf16[2,384,2048]{1,2,0:T(8,128)(2,1)}, bf16[2,384,2048]{1,2,0:T(8,128)(2,1)}, u32[]{:S(2)}, u32[]{:S(2)}) %collective-permute-start) | collective-permute-done | bytes 3145760 | tf_op jit(solution)/shard_map/ppermute | solution.py:12
  98.0 4.2 %fusion.26 = (bf16[2,768,1024]{1,2,0:T(8,128)(2,1)}, bf16[2,768,1024]{1,2,0:T(8,128)(2,1)S(1)}) fusion(bf16[2,384,2048]{1,2,0:T(8,128)(2,1)} %collective-permute-done, bf16[2,384,2048]{1,2,0:T(8,128)(2,1)} %copy.39), kind=kLoop, calls=%fused_computation.38 | loop fusion | flops 12582912 | bytes 12582912 | tf_op jit(solution)/shard_map/concatenate | solution.py:25
  102.1 7.9 %fusion.43 = f32[2,8,768,384]{2,3,1,0:T(8,128)} fusion(bf16[2,384,8,128]{1,3,2,0:T(8,128)(2,1)S(1)} %bitcast.74, bf16[2,768,8,128]{1,3,2,0:T(8,128)(2,1)S(1)} %bitcast.73), kind=kOutput, calls=%fused_computation.56 | convolution fusion | flops 1207959552 | bytes 23592960 | tf_op jit(solution)/shard_map/rfhd,rghd->rhfg/dot_general | solution.py:41
  110.0 12.0 %fusion.42 = (f32[2,8,384]{2,1,0:T(8,128)S(1)}, f32[2,8,384,768]{3,2,1,0:T(8,128)}) fusion(pred[768]{0:T(1024)(128)(4,1)S(1)} %fusion.33, bf16[2,384,8,128]{1,3,2,0:T(8,128)(2,1)} %bitcast.84, bf16[2,768,8,128]{1,3,2,0:T(8,128)(2,1)} %bitcast.80), kind=kOutput, calls=%fused_computation.55 | convolution fusion | flops 1226834688 | bytes 23618304 | tf_op jit(solution)/shard_map/sub | solution.py:37
  122.1 10.1 %fusion.6 = f32[2,8,768,128]{2,3,1,0:T(8,128)} fusion(bf16[2,384,8,128]{1,3,2,0:T(8,128)(2,1)S(1)} %bitcast.75, f32[2,8,384,768]{3,2,1,0:T(8,128)} %get-tuple-element.11, f32[2,8,384]{2,1,0:T(8,128)S(1)} %get-tuple-element.10), kind=kOutput, calls=%fused_computation.13 | convolution fusion | flops 1217396736 | bytes 26763264 | tf_op jit(solution)/shard_map/rhfg,rfhd->rghd/dot_general | solution.py:52
  132.2 46.9 %fusion.12 = f32[2,8,128,768]{3,2,1,0:T(8,128)} fusion(bf16[2,384,8,128]{1,3,2,0:T(8,128)(2,1)} %bitcast.85, f32[2,8,768,384]{2,3,1,0:T(8,128)} %fusion.43, f32[2,8,384,768]{3,2,1,0:T(8,128)} %get-tuple-element.11, f32[2,8,384]{2,1,0:T(8,128)S(1)} %get-tuple-element.10), kind=kOutput, calls=%fused_computation.20 | convolution fusion | flops 1240996608 | bytes 45637632 | tf_op jit(solution)/shard_map/rhfg,rfhd->rghd/dot_general | solution.py:49
  179.1 4.9 %fusion.17 = bf16[2,384,2048]{1,2,0:T(8,128)(2,1)} fusion(f32[2,768,1024]{1,2,0:T(8,128)} %bitcast.69, f32[2,768,1024]{1,2,0:T(8,128)} %bitcast.71), kind=kLoop, calls=%fused_computation.26 | loop fusion | flops 6291456 | bytes 15728640 | tf_op jit(solution)/shard_map/convert
  184.0 1.5 collective-permute-start.1
  185.5 46.1 %fusion.30 = bf16[2,8,128,384]{3,2,1,0:T(8,128)(2,1)S(1)} fusion(bf16[2,768,8,128]{1,3,2,0:T(8,128)(2,1)} %bitcast.81, f32[2,8,768,384]{2,3,1,0:T(8,128)} %fusion.43, f32[2,8,384,768]{3,2,1,0:T(8,128)} %get-tuple-element.11, f32[2,8,384]{2,1,0:T(8,128)S(1)} %get-tuple-element.10), kind=kOutput, calls=%fused_computation.41 | convolution fusion | flops 1241783040 | bytes 42491904 | tf_op jit(solution)/shard_map/rhfg,rghd->rfhd/dot_general | solution.py:46
  231.6 0.0 copy-start.3
  231.6 24.3 %collective-permute-done.1 = bf16[2,384,2048]{1,2,0:T(8,128)(2,1)} collective-permute-done((bf16[2,384,2048]{1,2,0:T(8,128)(2,1)}, bf16[2,384,2048]{1,2,0:T(8,128)(2,1)}, u32[]{:S(2)}, u32[]{:S(2)}) %collective-permute-start.1) | collective-permute-done | bytes 3145760 | tf_op jit(solution)/shard_map/ppermute | solution.py:12
  255.9 4.2 %fusion.16 = bf16[2,384,2048]{1,2,0:T(8,128)(2,1)S(1)} fusion(f32[2,768,1024]{1,2,0:T(8,128)} %bitcast.72, f32[2,768,1024]{1,2,0:T(8,128)} %bitcast.70, bf16[2,384,2048]{1,2,0:T(8,128)(2,1)} %collective-permute-done.1), kind=kLoop, calls=%fused_computation.24 | loop fusion | flops 6291456 | bytes 18874368 | tf_op jit(solution)/shard_map/convert_element_type | solution.py:65
  260.1 0.0 copy-start.1
  260.2 0.0 copy-done.3
  260.2 1.7 copy-done.1
  261.8 8.4 %fusion.18 = bf16[1024,3072]{0,1:T(8,128)(2,1)} fusion(bf16[2,384,1024]{2,1,0:T(8,128)(2,1)S(1)} %copy-done, bf16[2,384,2048]{1,2,0:T(8,128)(2,1)S(1)} %fusion.16, bf16[2,384,1024]{1,2,0:T(8,128)(2,1)S(1)} %bitcast.82), kind=kOutput, calls=%fused_computation.30 | convolution fusion | flops 4844421120 | bytes 12582912 | tf_op jit(solution)/shard_map/dot_general | solution.py:73
  270.3 0.0 reduce-scatter.5.cloned.1.call-update
  270.3 0.0 reduce-scatter.7.cloned.1.call-start
  270.4 59.4 %reduce-scatter.5.cloned.1.call-done = bf16[256,3072]{0,1:T(8,128)(2,1)} async-done(((bf16[1024,3072]{0,1:T(8,128)(2,1)}), bf16[256,3072]{0,1:T(8,128)(2,1)}) %reduce-scatter.5.cloned.1.call-update) | async-done | bytes 1572880 | tf_op jit(solution)/shard_map/reduce_scatter | solution.py:76
  329.8 2.6 copy.37
  332.3 0.0 reduce-scatter.7.cloned.1.call-update
  332.4 2.1 copy.29
  334.5 1.6 copy.44
  336.1 0.0 copy-start.4
  336.1 4.9 %copy.31 = bf16[2,384,2048]{2,1,0:T(8,128)(2,1)} copy(bf16[2,384,2048]{1,2,0:T(8,128)(2,1)} %copy-done.1) | data formatting | bytes 6291456 | tf_op jit(solution)/shard_map/convert_element_type | solution.py:65
  341.0 0.0 copy-done.4
  341.0 9.0 %fusion.27 = bf16[768,1024]{1,0:T(8,128)(2,1)} fusion(bf16[1024,3072]{1,0:T(8,128)(2,1)} %param.4, bf16[768,2048]{1,0:T(8,128)(2,1)} %bitcast.79, bf16[768,1024]{1,0:T(8,128)(2,1)S(1)} %bitcast.86), kind=kOutput, calls=%fused_computation.40 | convolution fusion | flops 4842061824 | bytes 12582912 | tf_op jit(solution)/shard_map/dot_general | solution.py:68
  350.0 49.0 %reduce-scatter.7.cloned.1.call-done = bf16[32,3072]{1,0:T(8,128)(2,1)} async-done(((bf16[256,3072]{1,0:T(8,128)(2,1)}), bf16[32,3072]{1,0:T(8,128)(2,1)}) %reduce-scatter.7.cloned.1.call-update) | async-done | bytes 196624
  399.0 2.1 copy.38
  401.1 1.3 convert_multiply_fusion
  402.3 1.2 copy.32
  (1 shorter events, 0.0 us)
Async XLA Ops:
  7.2 1.4 copy-start
  7.2 322.6 %reduce-scatter.5.cloned.1.call-start = ((), (), s32[]{:S(2)}) async-start(), calls=%async_computation.2 | async-start | bytes 7864320 | tf_op jit(solution)/shard_map/reduce_scatter | solution.py:76
  16.6 2.1 copy-start.2
  25.4 72.6 %collective-permute-start = (bf16[2,384,2048]{1,2,0:T(8,128)(2,1)}, bf16[2,384,2048]{1,2,0:T(8,128)(2,1)}, u32[]{:S(2)}, u32[]{:S(2)}) collective-permute-start(bf16[2,384,2048]{1,2,0:T(8,128)(2,1)} %copy.39), channel_id=1, source_target_pairs={{0,1},{1,2},{2,3},{3,4},{4,5},{5,6},{6,7},{8,9},{9,10},{10,11},{11... | collective-permute-start | bytes 9437192 | tf_op jit(solution)/shard_map/ppermute | solution.py:12
  184.0 71.9 %collective-permute-start.1 = (bf16[2,384,2048]{1,2,0:T(8,128)(2,1)}, bf16[2,384,2048]{1,2,0:T(8,128)(2,1)}, u32[]{:S(2)}, u32[]{:S(2)}) collective-permute-start(bf16[2,384,2048]{1,2,0:T(8,128)(2,1)} %fusion.17), channel_id=1, source_target_pairs={{1,0},{2,1},{3,2},{4,3},{5,4},{6,5},{7,6},{9,8},{10,9},{11,10},{12... | collective-permute-start | bytes 9437192 | tf_op jit(solution)/shard_map/ppermute | solution.py:12
  231.6 28.5 %copy-start.3 = (bf16[2,8,128,384]{3,2,1,0:T(8,128)(2,1)}, bf16[2,8,128,384]{3,2,1,0:T(8,128)(2,1)S(1)}, u32[]{:S(2)}) copy-start(bf16[2,8,128,384]{3,2,1,0:T(8,128)(2,1)S(1)} %fusion.30) | copy-start | bytes 4718596
  260.1 1.7 copy-start.1
  270.3 128.7 %reduce-scatter.7.cloned.1.call-start = ((), (), s32[]{:S(2)}) async-start(), calls=%async_computation.3 | async-start | bytes 1769472
  336.1 4.9 %copy-start.4 = (bf16[96,8,8,128]{3,1,2,0:T(8,128)(2,1)S(1)}, bf16[96,8,8,128]{3,1,2,0:T(8,128)(2,1)}, u32[]{:S(2)}) copy-start(bf16[96,8,8,128]{3,1,2,0:T(8,128)(2,1)} %copy.44) | copy-start | bytes 4718596
Sparse Core Ops, SparseCore 0:
  270.4 59.2 reduce-scatter.4
  333.2 65.7 reduce-scatter.6
where the time goes:
time: 411 us; the launch traced here: 410 us
  waiting for transfers between devices  191 us (46%)
  matrix products  149 us (36%)
  local copies, waits for them, and re-layouts  33.5 us (8%)
  other arithmetic  14.5 us (4%)
  between operations  14.1 us (3%)
  starting transfers between devices  8.22 us (2%)
    ppermute x2, waiting for transfers between devices, passed_along(): lax.ppermute(value, axis, [(source, source + steps) for source in range(f...  83 us
    reduce_scatter x1, waiting for transfers between devices, local(): lax.psum_scatter(full_terms.astype(jnp.bfloat16), 'stream', scatter_dimen...  59.4 us
    unnamed x3, waiting for transfers between devices  49 us
    dot_general x1, matrix products, local(): jnp.einsum('rhfg,rfhd->rghd', dscore, query_heads, preferred_element_type...  46.9 us
    dot_general x1, matrix products, local(): jnp.einsum('rhfg,rghd->rfhd', dscore, key_heads, preferred_element_type=j...  46.1 us
    unnamed x16, local copies, waits for them, and re-layouts  19.9 us
    sub x1, matrix products, local(): expo = jnp.exp(scores - peak)  12 us
    dot_general x1, matrix products, local(): jnp.einsum('rhfg,rfhd->rghd', prob_b, grad_heads, preferred_element_type=...  10.1 us
  transfers between devices with their start and end apart: 4, of which 4 were waited for; matrix products, arithmetic and copies ran while one was open for 17% of the time, Pallas kernels for 0%

commit v1 on v0

v1 whole, which is shorter than its diff:
```python
import functools

import jax
import jax.numpy as jnp
from jax import lax
from jax.experimental import pallas as pl
from jax.experimental.pallas import tpu as pltpu
from jax.sharding import PartitionSpec as P

HEADS = 8
LOG2E = 1.4426950408889634
NT = (((1,), (1,)), ((), ()))
TN = (((0,), (0,)), ((), ()))


def passed_along(value, axis, steps):
    count = lax.axis_size(axis)
    first, last = (max(0, -steps), min(count, count - steps))
    return lax.ppermute(value, axis, [(source, source + steps) for source in range(first, last)])


def dot(a, b, dims=(((1,), (0,)), ((), ()))):
    return lax.dot_general(a, b, dims, preferred_element_type=jnp.float32)


def attention_kernel(width, qkv_ref, prev_ref, grad_ref, own_ref, earlier_ref):
    head_size = width // HEADS
    scale = head_size ** (-0.5)
    bias = jnp.where(lax.axis_index("tm") > 0, 0.0, -1e30).astype(jnp.float32)

    def columns(section):
        start = section * width + pl.program_id(0) * head_size
        return pl.ds(pl.multiple_of(start, head_size), head_size)

    q = qkv_ref[:, columns(0)]
    k_own = qkv_ref[:, columns(1)]
    v_own = qkv_ref[:, columns(2)]
    k_prev = prev_ref[:, columns(0)]
    v_prev = prev_ref[:, columns(1)]
    grad = grad_ref[:, columns(0)]
    s_own = dot(k_own, q, NT)
    s_prev = dot(k_prev, q, NT) + bias
    peak = jnp.maximum(jnp.max(s_own, 0, keepdims=True), jnp.max(s_prev, 0, keepdims=True))
    e_own = jnp.exp2((s_own - peak) * (scale * LOG2E))
    e_prev = jnp.exp2((s_prev - peak) * (scale * LOG2E))
    total = jnp.sum(e_own, 0, keepdims=True) + jnp.sum(e_prev, 0, keepdims=True)
    inverse = 1.0 / total
    p_own = e_own * inverse
    p_prev = e_prev * inverse
    dp_own = dot(v_own, grad, NT)
    dp_prev = dot(v_prev, grad, NT)
    delta = jnp.sum(p_own * dp_own, 0, keepdims=True) + jnp.sum(p_prev * dp_prev, 0, keepdims=True)
    ds_own = (p_own * (dp_own - delta)).astype(jnp.bfloat16)
    ds_prev = (p_prev * (dp_prev - delta)).astype(jnp.bfloat16)
    dq = dot(ds_own, k_own, TN) + dot(ds_prev, k_prev, TN)
    own_ref[:, columns(0)] = (dq * scale).astype(jnp.bfloat16)
    own_ref[:, columns(1)] = (dot(ds_own, q) * scale).astype(jnp.bfloat16)
    own_ref[:, columns(2)] = dot(p_own.astype(jnp.bfloat16), grad).astype(jnp.bfloat16)
    earlier_ref[:, columns(0)] = (dot(ds_prev, q) * scale).astype(jnp.bfloat16)
    earlier_ref[:, columns(1)] = dot(p_prev.astype(jnp.bfloat16), grad).astype(jnp.bfloat16)


def attention(qkv, prev, grad):
    frames, width = grad.shape
    whole = lambda a: pl.BlockSpec(a.shape, lambda h: (0, 0))
    outs = (
        jax.ShapeDtypeStruct((frames, 3 * width), jnp.bfloat16),
        jax.ShapeDtypeStruct((frames, 2 * width), jnp.bfloat16),
    )
    return pl.pallas_call(
        functools.partial(attention_kernel, width),
        grid=(HEADS,),
        in_specs=[whole(qkv), whole(prev), whole(grad)],
        out_specs=[whole(o) for o in outs],
        out_shape=outs,
        cost_estimate=pl.CostEstimate(
            flops=20 * frames * frames * width,
            bytes_accessed=22 * frames * width,
            transcendentals=2 * HEADS * frames * frames,
        ),
    )(qkv, prev, grad)


def local(frames_in, w_qkv, grad_out):
    records, frame_count, width = frames_in.shape
    w_kv = w_qkv[:, width:]
    total_frames = records * frame_count * lax.axis_size("stream") * lax.axis_size("tm")
    before = [passed_along(frames_in[r], "tm", 1) for r in range(records)]
    own_in, own, earlier, returned = [], [], [], []
    for r in range(records):
        qkv = dot(frames_in[r], w_qkv).astype(jnp.bfloat16)
        prev = dot(before[r], w_kv).astype(jnp.bfloat16)
        d_own, d_earlier = attention(qkv, prev, grad_out[r])
        back = dot(d_earlier, w_kv, NT).astype(jnp.bfloat16)
        returned.append(passed_along(back, "tm", -1))
        own.append(d_own)
        earlier.append(d_earlier)
    q_terms = sum(dot(frames_in[r], own[r][:, :width], TN) for r in range(records))
    kv_terms = sum(
        dot(frames_in[r], own[r][:, width:], TN) + dot(before[r], earlier[r], TN)
        for r in range(records)
    )
    terms = jnp.concatenate([q_terms, kv_terms], 1).astype(jnp.bfloat16)
    reduced = lax.psum_scatter(terms, ("stream", "tm"), scatter_dimension=0, tiled=True)
    grad_w = reduced.astype(jnp.float32) * float(total_frames) ** (-0.5)
    grad_in = jnp.stack(
        [
            (dot(own[r], w_qkv, NT) + returned[r].astype(jnp.float32)).astype(jnp.bfloat16)
            for r in range(records)
        ]
    )
    return (grad_in, grad_w)


def solution(mesh):
    return jax.shard_map(
        local,
        mesh=mesh,
        in_specs=(P("stream", "tm", None), P(), P("stream", "tm", None)),
        out_specs=(P("stream", "tm", None), P(("stream", "tm"), None)),
        check_vma=False,
    )
```

time: 411 us -> 247 us (0.60)
  waiting for transfers between devices: 191 us -> 99.2 us
  matrix products: 149 us -> 68.3 us
  Pallas kernels: 0 us -> 31.4 us
  local copies, waits for them, and re-layouts: 33.5 us -> 15.5 us
  other arithmetic: 14.5 us -> 4.74 us
  starting transfers between devices: 8.22 us -> 13 us
    dot_general x7 -> x14, matrix products: 137 us -> 68.3 us  [dot(): return lax.dot_general(a, b, dims, preferred_element_type=jnp.float32)]
    reduce_scatter x1 -> x0, waiting for transfers between devices: 59.4 us -> none  [local(): lax.psum_scatter(full_terms.astype(jnp.bfloat16), 'stream', scatter_dimen...]
    ppermute x2 -> x4, waiting for transfers between devices: 83 us -> 28.4 us  [passed_along(): lax.ppermute(value, axis, [(source, source + steps) for source in range(f...]
    pallas_call x0 -> x2, Pallas kernels: none -> 31.4 us  [attention(): pl.pallas_call(functools.partial(attention_kernel, width), grid=(HEADS,),...]
    unnamed x3 -> x2, waiting for transfers between devices: 49 us -> 70.8 us
    sub x1 -> x0, matrix products: 12 us -> none  [local(): expo = jnp.exp(scores - peak)]
    unnamed x16 -> x39, local copies, waits for them, and re-layouts: 19.9 us -> 12.6 us
    convert_element_type x2 -> x0, local copies, waits for them, and re-layouts: 7.03 us -> none  [the longest x1 4.88 us: local(): summed = (own_part + returned).astype(jnp.bfloat16)]
  transfers between devices with their start and end apart: 4 -> 5, of which waited for: 4 -> 4; matrix products, arithmetic and copies ran while one was open for 17% -> 16% of each run, Pallas kernels for 0% -> 6%
where the time goes in v1:
time: 247 us; the launch traced here: 246 us
  waiting for transfers between devices  99.2 us (40%)
  matrix products  68.3 us (28%)
  Pallas kernels  31.4 us (13%)
  local copies, waits for them, and re-layouts  15.5 us (6%)
  between operations  14.2 us (6%)
  starting transfers between devices  13 us (5%)
  other arithmetic  4.74 us (2%)
    unnamed x2, waiting for transfers between devices  70.8 us
    dot_general x14, matrix products, dot(): return lax.dot_general(a, b, dims, preferred_element_type=jnp.float32)  68.3 us
    pallas_call x2, Pallas kernels, attention(): pl.pallas_call(functools.partial(attention_kernel, width), grid=(HEADS,),...  31.4 us
    ppermute x4, waiting for transfers between devices, passed_along(): lax.ppermute(value, axis, [(source, source + steps) for source in range(f...  28.4 us
    ppermute x4, starting transfers between devices, passed_along(): lax.ppermute(value, axis, [(source, source + steps) for source in range(f...  13 us
    unnamed x39, local copies, waits for them, and re-layouts  12.6 us
  transfers between devices with their start and end apart: 5, of which 4 were waited for; matrix products, arithmetic and copies ran while one was open for 16% of the time, Pallas kernels for 6%

profile of v1, /device:TPU:0, one launch (start us, length us, event | category | flops | bytes accessed | tf_op | source)
XLA Modules:
  0.0 246.3 jit_solution(18082642909284721227)
XLA Ops:
  7.2 0.0 copy-start.1
  7.2 0.0 reduce-scatter.4.cloned.1.call-start
  7.2 0.0 slice-start.2
  7.2 1.6 slice_bitcast_fusion.3
  8.9 5.1 %collective-permute-start = (bf16[384,1024]{1,0:T(8,128)(2,1)S(1)}, bf16[384,1024]{1,0:T(8,128)(2,1)S(1)}, u32[]{:S(2)}, u32[]{:S(2)}) collective-permute-start(bf16[384,1024]{1,0:T(8,128)(2,1)S(1)} %get-tuple-element.16), channel_id=1, source_target_pairs={{0,1},{1,2},{2,3},{3,4},{4,5},{5,6},{6,7},{8,9},{9,10},{10,11},{11... | collective-permute-start | bytes 2359304 | tf_op jit(solution)/shard_map/ppermute | solution.py:19
  14.0 0.0 copy-start.8
  14.0 0.0 slice-start.3
  14.0 4.5 %collective-permute-start.2 = (bf16[384,1024]{1,0:T(8,128)(2,1)S(1)}, bf16[384,1024]{1,0:T(8,128)(2,1)}, u32[]{:S(2)}, u32[]{:S(2)}) collective-permute-start(bf16[384,1024]{1,0:T(8,128)(2,1)S(1)} %get-tuple-element.17), channel_id=1, source_target_pairs={{0,1},{1,2},{2,3},{3,4},{4,5},{5,6},{6,7},{8,9},{9,10},{10,11},{11... | collective-permute-start | bytes 2359304 | tf_op jit(solution)/shard_map/ppermute | solution.py:19
  18.5 0.0 copy-done.1
  18.5 6.6 %convolution_convert_fusion.1.qkv_ref = bf16[384,3072]{1,0:T(8,128)(2,1)} fusion(bf16[1024,3072]{1,0:T(8,128)(2,1)} %param.4, bf16[2,384,1024]{2,1,0:T(8,128)(2,1)S(1)} %copy-done.1), kind=kOutput, calls=%fused_computation.3 | convolution fusion | flops 2417098752 | bytes 9437184 | tf_op jit(solution)/shard_map/dot_general | solution.py:23
  25.2 0.0 copy-done.8
  25.2 1.3 slice_bitcast_fusion.2
  26.4 0.0 slice-done.2
  26.4 0.0 slice-done.3
  26.4 3.9 %convolution_convert_fusion.qkv_ref = bf16[384,3072]{1,0:T(8,128)(2,1)} fusion(bf16[1024,3072]{1,0:T(8,128)(2,1)S(1)} %bitcast.40, bf16[2,384,1024]{2,1,0:T(8,128)(2,1)S(1)} %copy-done.1), kind=kOutput, calls=%fused_computation.2 | convolution fusion | flops 2417098752 | bytes 9437184 | tf_op jit(solution)/shard_map/dot_general | solution.py:23
  30.3 1.5 collective-permute-done
  31.8 2.9 %convolution_convert_fusion.3.prev_ref = bf16[384,2048]{1,0:T(8,128)(2,1)} fusion(bf16[384,1024]{1,0:T(8,128)(2,1)S(1)} %collective-permute-done, bf16[1024,3072]{1,0:T(8,128)(2,1)S(1)} %bitcast.40), kind=kOutput, calls=%fused_computation.7 | convolution fusion | flops 1611399168 | bytes 6553600 | tf_op jit(solution)/shard_map/dot_general | solution.py:23
  34.8 15.7 %shard_map.50 = (bf16[384,3072]{1,0:T(8,128)(2,1)}, bf16[384,2048]{1,0:T(8,128)(2,1)}) custom-call(bf16[384,3072]{1,0:T(8,128)(2,1)} %convolution_convert_fusion.1.qkv_ref, bf16[384,2048]{1,0:T(8,128)(2,1)} %convolution_convert_fusion.3.prev_ref, bf16[384,1024]{1,0:T(8,128)(2,1)} %get-tuple-element.14.grad_ref), custom_call_target="tpu_custom_call" | custom-call | flops 3019898880 | bytes 8650752 | tf_op jit(solution)/shard_map/pallas_call | solution.py:70
  50.5 0.0 copy-start.3
  50.5 0.0 slice-start.4
  50.5 4.5 %fusion.21 = f32[1024,1024]{1,0:T(8,128)} fusion(bf16[384,3072]{1,0:T(8,128)(2,1)} %get-tuple-element.6, bf16[2,384,1024]{2,1,0:T(8,128)(2,1)S(1)} %copy-done.1), kind=kOutput, calls=%fused_computation.28 | convolution fusion | flops 805306368 | bytes 5767168 | tf_op jit(solution)/shard_map/dot_general | solution.py:23
  55.0 0.0 copy-done.3
  55.0 5.7 %fusion.10 = f32[2048,1024]{1,0:T(8,128)} fusion(bf16[384,3072]{1,0:T(8,128)(2,1)S(1)} %copy-done.3, bf16[2,384,1024]{2,1,0:T(8,128)(2,1)S(1)} %copy-done.1), kind=kOutput, calls=%fused_computation.19 | convolution fusion | flops 1610612736 | bytes 10747904 | tf_op jit(solution)/shard_map/dot_general | solution.py:23
  60.7 0.0 collective-permute-done.2
  60.7 0.0 slice-done.4
  60.7 0.0 slice-done.5
  60.7 4.1 %convolution_convert_fusion.2.prev_ref = bf16[384,2048]{1,0:T(8,128)(2,1)} fusion(bf16[384,1024]{1,0:T(8,128)(2,1)} %collective-permute-done.2, bf16[1024,3072]{1,0:T(8,128)(2,1)S(1)} %bitcast.42), kind=kOutput, calls=%fused_computation.6 | convolution fusion | flops 1611399168 | bytes 6553600 | tf_op jit(solution)/shard_map/dot_general | solution.py:23
  64.8 15.7 %shard_map.51 = (bf16[384,3072]{1,0:T(8,128)(2,1)}, bf16[384,2048]{1,0:T(8,128)(2,1)}) custom-call(bf16[384,3072]{1,0:T(8,128)(2,1)} %convolution_convert_fusion.qkv_ref, bf16[384,2048]{1,0:T(8,128)(2,1)} %convolution_convert_fusion.2.prev_ref, bf16[384,1024]{1,0:T(8,128)(2,1)} %get-tuple-element.15.grad_ref), custom_call_target="tpu_custom_call" | custom-call | flops 3019898880 | bytes 8650752 | tf_op jit(solution)/shard_map/pallas_call | solution.py:70
  80.5 0.0 copy-start
  80.5 7.2 %fusion.8 = f32[2048,1024]{1,0:T(8,128)} fusion(bf16[384,3072]{1,0:T(8,128)(2,1)} %get-tuple-element.8, bf16[2,384,1024]{2,1,0:T(8,128)(2,1)S(1)} %copy-done.1), kind=kOutput, calls=%fused_computation.17 | convolution fusion | flops 1610612736 | bytes 10747904 | tf_op jit(solution)/shard_map/dot_general | solution.py:23
  87.7 0.0 copy-done
  87.7 0.0 copy-start.6
  87.7 4.0 %fusion.7 = bf16[1024,1024]{0,1:T(8,128)(2,1)} fusion(f32[1024,1024]{1,0:T(8,128)S(1)} %copy-done, bf16[384,3072]{1,0:T(8,128)(2,1)} %get-tuple-element.8, bf16[2,384,1024]{2,1,0:T(8,128)(2,1)S(1)} %copy-done.1), kind=kOutput, calls=%fused_computation.14 | convolution fusion | flops 807403520 | bytes 7864320 | tf_op jit(solution)/shard_map/dot_general | solution.py:23
  91.7 0.0 copy-done.6
  91.7 5.7 %fusion.23 = f32[2048,1024]{1,0:T(8,128)} fusion(bf16[384,2048]{1,0:T(8,128)(2,1)S(1)} %copy-done.6, bf16[384,1024]{1,0:T(8,128)(2,1)S(1)} %collective-permute-done), kind=kOutput, calls=%fused_computation.34 | convolution fusion | flops 1610612736 | bytes 10747904 | tf_op jit(solution)/shard_map/dot_general | solution.py:23
  97.4 0.0 slice-done
  97.4 0.0 slice-done.1
  97.4 10.2 %fusion = bf16[1024,2048]{0,1:T(8,128)(2,1)S(1)} fusion(f32[2048,1024]{1,0:T(8,128)} %fusion.8, bf16[384,2048]{1,0:T(8,128)(2,1)} %get-tuple-element.9, bf16[384,1024]{1,0:T(8,128)(2,1)} %collective-permute-done.2, f32[2048,1024]{1,0:T(8,128)S(1)} %bitcast.38, f32[2048,1024]{1,0:T(8,128)} %fusion.23), kind=kOutput, calls=%fused_computation.5 | convolution fusion | flops 1619001344 | bytes 31719424 | tf_op jit(solution)/shard_map/dot_general | solution.py:23
  107.5 0.0 copy-done.2
  107.5 3.3 %pad_maximum_fusion = bf16[1024,3072]{0,1:T(8,128)(2,1)} fusion(bf16[1024,2048]{0,1:T(8,128)(2,1)S(1)} %fusion, bf16[1024,1024]{0,1:T(8,128)(2,1)S(1)} %copy-done.2), kind=kLoop, calls=%fused_computation.1 | loop fusion | flops 12582912 | bytes 12582912 | tf_op jit(solution)/shard_map/concatenate | solution.py:103
  110.9 8.6 %copy.7 = bf16[1024,3072]{1,0:T(8,128)(2,1)} copy(bf16[1024,3072]{0,1:T(8,128)(2,1)} %pad_maximum_fusion) | data formatting | bytes 12582912
  119.5 0.0 reduce-scatter.4.cloned.1.call-update
  119.5 1.4 copy-done.7
  120.9 4.2 %fusion.12 = bf16[384,1024]{1,0:T(8,128)(2,1)S(1)} fusion(bf16[384,2048]{1,0:T(8,128)(2,1)S(1)} %copy-done.7, bf16[1024,3072]{1,0:T(8,128)(2,1)} %param.4), kind=kOutput, calls=%fused_computation.23 | convolution fusion | flops 1611005952 | bytes 6553600 | tf_op jit(solution)/shard_map/dot_general | solution.py:23
  125.1 0.0 copy-start.4
  125.1 0.0 slice-start.7
  125.1 1.8 collective-permute-start.1
  126.9 0.0 copy-done.9
  126.9 4.1 %fusion.15 = bf16[384,1024]{1,0:T(8,128)(2,1)S(1)} fusion(bf16[384,2048]{1,0:T(8,128)(2,1)S(1)} %copy-done.9, bf16[1024,3072]{1,0:T(8,128)(2,1)} %param.4), kind=kOutput, calls=%fused_computation.24 | convolution fusion | flops 1611005952 | bytes 6553600 | tf_op jit(solution)/shard_map/dot_general | solution.py:23
  131.0 0.0 copy-start.5
  131.0 1.6 collective-permute-start.3
  132.6 15.6 %collective-permute-done.1 = bf16[384,1024]{1,0:T(8,128)(2,1)S(1)} collective-permute-done((bf16[384,1024]{1,0:T(8,128)(2,1)S(1)}, bf16[384,1024]{1,0:T(8,128)(2,1)S(1)}, u32[]{:S(2)}, u32[]{:S(2)}) %collective-permute-start.1) | collective-permute-done | bytes 786464 | tf_op jit(solution)/shard_map/ppermute | solution.py:19
  148.2 0.0 slice-done.6
  148.2 0.0 copy-done.4
  148.2 0.0 slice-done.7
  148.2 2.7 %fusion.18 = bf16[1,384,1024]{2,1,0:T(8,128)(2,1)S(1)} fusion(bf16[384,1024]{1,0:T(8,128)(2,1)S(1)} %collective-permute-done.1, bf16[384,3072]{1,0:T(8,128)(2,1)S(1)} %copy-done.4, bf16[1024,3072]{1,0:T(8,128)(2,1)S(1)} %bitcast.44), kind=kOutput, calls=%fused_computation.25 | convolution fusion | flops 2417098752 | bytes 10223616 | tf_op jit(solution)/shard_map/dot_general | solution.py:23
  150.8 11.3 %collective-permute-done.3 = bf16[384,1024]{1,0:T(8,128)(2,1)S(1)} collective-permute-done((bf16[384,1024]{1,0:T(8,128)(2,1)S(1)}, bf16[384,1024]{1,0:T(8,128)(2,1)S(1)}, u32[]{:S(2)}, u32[]{:S(2)}) %collective-permute-start.3) | collective-permute-done | bytes 786464 | tf_op jit(solution)/shard_map/ppermute | solution.py:19
  162.2 0.0 copy-done.5
  162.2 2.7 %fusion.19 = bf16[1,384,1024]{2,1,0:T(8,128)(2,1)S(1)} fusion(bf16[384,1024]{1,0:T(8,128)(2,1)S(1)} %collective-permute-done.3, bf16[384,3072]{1,0:T(8,128)(2,1)S(1)} %copy-done.5, bf16[1024,3072]{1,0:T(8,128)(2,1)S(1)} %bitcast.44), kind=kOutput, calls=%fused_computation.26 | convolution fusion | flops 2417098752 | bytes 10223616 | tf_op jit(solution)/shard_map/dot_general | solution.py:23
  164.8 1.3 pad_maximum_fusion.1
  166.1 70.7 %reduce-scatter.4.cloned.1.call-done = bf16[32,3072]{1,0:T(8,128)(2,1)} async-done(((bf16[1024,3072]{1,0:T(8,128)(2,1)}), bf16[32,3072]{1,0:T(8,128)(2,1)}) %reduce-scatter.4.cloned.1.call-update) | async-done | bytes 196624
  236.9 1.3 copy.8
  238.2 0.1 convert_multiply_fusion
  238.3 1.2 copy.6
  (11 shorter events, 0.0 us)
Async XLA Ops:
  7.2 11.4 %copy-start.1 = (bf16[2,384,1024]{2,1,0:T(8,128)(2,1)S(1)}, bf16[2,384,1024]{2,1,0:T(8,128)(2,1)}, u32[]{:S(2)}) copy-start(bf16[2,384,1024]{2,1,0:T(8,128)(2,1)} %param.3) | copy-start | bytes 4718596
  7.2 229.7 %reduce-scatter.4.cloned.1.call-start = ((), (), s32[]{:S(2)}) async-start(), calls=%async_computation.1 | async-start | bytes 6488064
  7.2 19.2 %slice-start.2 = ((s8[6291456]{0:T(1024)(128)(4,1)}), s8[4194304]{0:T(1024)(128)(4,1)S(1)}, s32[]{:S(2)}) async-start(s8[6291456]{0:T(1024)(128)(4,1)} %bitcast.39), calls=%async_computation.4 | async-start | bytes 8388608
  8.9 23.0 %collective-permute-start = (bf16[384,1024]{1,0:T(8,128)(2,1)S(1)}, bf16[384,1024]{1,0:T(8,128)(2,1)S(1)}, u32[]{:S(2)}, u32[]{:S(2)}) collective-permute-start(bf16[384,1024]{1,0:T(8,128)(2,1)S(1)} %get-tuple-element.16), channel_id=1, source_target_pairs={{0,1},{1,2},{2,3},{3,4},{4,5},{5,6},{6,7},{8,9},{9,10},{10,11},{11... | collective-permute-start | bytes 2359304 | tf_op jit(solution)/shard_map/ppermute | solution.py:19
  14.0 11.2 %copy-start.8 = (bf16[2,384,1024]{2,1,0:T(8,128)(2,1)S(1)}, bf16[2,384,1024]{2,1,0:T(8,128)(2,1)}, u32[]{:S(2)}) copy-start(bf16[2,384,1024]{2,1,0:T(8,128)(2,1)} %param.5) | copy-start | bytes 4718596
  14.0 12.5 %slice-start.3 = ((s8[6291456]{0:T(1024)(128)(4,1)}), s8[2097152]{0:T(1024)(128)(4,1)S(1)}, s32[]{:S(2)}) async-start(s8[6291456]{0:T(1024)(128)(4,1)} %bitcast.39), calls=%async_computation.5 | async-start | bytes 4194304
  14.0 46.7 %collective-permute-start.2 = (bf16[384,1024]{1,0:T(8,128)(2,1)S(1)}, bf16[384,1024]{1,0:T(8,128)(2,1)}, u32[]{:S(2)}, u32[]{:S(2)}) collective-permute-start(bf16[384,1024]{1,0:T(8,128)(2,1)S(1)} %get-tuple-element.17), channel_id=1, source_target_pairs={{0,1},{1,2},{2,3},{3,4},{4,5},{5,6},{6,7},{8,9},{9,10},{10,11},{11... | collective-permute-start | bytes 2359304 | tf_op jit(solution)/shard_map/ppermute | solution.py:19
  50.5 4.5 %copy-start.3 = (bf16[384,3072]{1,0:T(8,128)(2,1)S(1)}, bf16[384,3072]{1,0:T(8,128)(2,1)}, u32[]{:S(2)}) copy-start(bf16[384,3072]{1,0:T(8,128)(2,1)} %get-tuple-element.6) | copy-start | bytes 7077892
  50.5 10.2 %slice-start.4 = ((s8[6291456]{0:T(1024)(128)(4,1)}), s8[4194304]{0:T(1024)(128)(4,1)S(1)}, s32[]{:S(2)}) async-start(s8[6291456]{0:T(1024)(128)(4,1)} %bitcast.41), calls=%async_computation.6 | async-start | bytes 8388608
  55.0 5.7 %slice-start.5 = ((s8[6291456]{0:T(1024)(128)(4,1)}), s8[2097152]{0:T(1024)(128)(4,1)S(1)}, s32[]{:S(2)}) async-start(s8[6291456]{0:T(1024)(128)(4,1)} %bitcast.41), calls=%async_computation.7 | async-start | bytes 4194304
  80.5 7.2 %copy-start = (f32[1024,1024]{1,0:T(8,128)S(1)}, f32[1024,1024]{1,0:T(8,128)}, u32[]{:S(2)}) copy-start(f32[1024,1024]{1,0:T(8,128)} %fusion.21) | copy-start | bytes 12582916
  87.7 4.0 %copy-start.6 = (bf16[384,2048]{1,0:T(8,128)(2,1)S(1)}, bf16[384,2048]{1,0:T(8,128)(2,1)}, u32[]{:S(2)}) copy-start(bf16[384,2048]{1,0:T(8,128)(2,1)} %get-tuple-element.7) | copy-start | bytes 4718596
  87.7 9.7 %slice-start = ((s8[8388608]{0:T(1024)(128)(4,1)}), s8[4194304]{0:T(1024)(128)(4,1)S(1)}, s32[]{:S(2)}) async-start(s8[8388608]{0:T(1024)(128)(4,1)} %bitcast.37), calls=%async_computation.2 | async-start | bytes 8388608
  91.7 5.7 %slice-start.1 = ((s8[8388608]{0:T(1024)(128)(4,1)}), s8[4194304]{0:T(1024)(128)(4,1)S(1)}, s32[]{:S(2)}) async-start(s8[8388608]{0:T(1024)(128)(4,1)} %bitcast.37), calls=%async_computation.3 | async-start | bytes 8388608
  97.4 10.2 %copy-start.2 = (bf16[1024,1024]{0,1:T(8,128)(2,1)S(1)}, bf16[1024,1024]{0,1:T(8,128)(2,1)}, u32[]{:S(2)}) copy-start(bf16[1024,1024]{0,1:T(8,128)(2,1)} %fusion.7) | copy-start | bytes 6291460
  119.5 1.4 copy-start.7
  120.9 6.0 %copy-start.9 = (bf16[384,2048]{1,0:T(8,128)(2,1)S(1)}, bf16[384,2048]{1,0:T(8,128)(2,1)}, u32[]{:S(2)}) copy-start(bf16[384,2048]{1,0:T(8,128)(2,1)} %get-tuple-element.9) | copy-start | bytes 4718596
  120.9 27.2 %slice-start.6 = ((s8[6291456]{0:T(1024)(128)(4,1)}), s8[4194304]{0:T(1024)(128)(4,1)S(1)}, s32[]{:S(2)}) async-start(s8[6291456]{0:T(1024)(128)(4,1)} %bitcast.43), calls=%async_computation.8 | async-start | bytes 8388608
  125.1 23.1 %copy-start.4 = (bf16[384,3072]{1,0:T(8,128)(2,1)S(1)}, bf16[384,3072]{1,0:T(8,128)(2,1)}, u32[]{:S(2)}) copy-start(bf16[384,3072]{1,0:T(8,128)(2,1)} %get-tuple-element.6) | copy-start | bytes 7077892
  125.1 23.1 %slice-start.7 = ((s8[6291456]{0:T(1024)(128)(4,1)}), s8[2097152]{0:T(1024)(128)(4,1)S(1)}, s32[]{:S(2)}) async-start(s8[6291456]{0:T(1024)(128)(4,1)} %bitcast.43), calls=%async_computation.9 | async-start | bytes 4194304
  125.1 23.0 %collective-permute-start.1 = (bf16[384,1024]{1,0:T(8,128)(2,1)S(1)}, bf16[384,1024]{1,0:T(8,128)(2,1)S(1)}, u32[]{:S(2)}, u32[]{:S(2)}) collective-permute-start(bf16[384,1024]{1,0:T(8,128)(2,1)S(1)} %fusion.12), channel_id=1, source_target_pairs={{1,0},{2,1},{3,2},{4,3},{5,4},{6,5},{7,6},{9,8},{10,9},{11,10},{12... | collective-permute-start | bytes 2359304 | tf_op jit(solution)/shard_map/ppermute | solution.py:19
  131.0 31.2 %copy-start.5 = (bf16[384,3072]{1,0:T(8,128)(2,1)S(1)}, bf16[384,3072]{1,0:T(8,128)(2,1)}, u32[]{:S(2)}) copy-start(bf16[384,3072]{1,0:T(8,128)(2,1)} %get-tuple-element.8) | copy-start | bytes 7077892
  131.0 31.2 %collective-permute-start.3 = (bf16[384,1024]{1,0:T(8,128)(2,1)S(1)}, bf16[384,1024]{1,0:T(8,128)(2,1)S(1)}, u32[]{:S(2)}, u32[]{:S(2)}) collective-permute-start(bf16[384,1024]{1,0:T(8,128)(2,1)S(1)} %fusion.15), channel_id=1, source_target_pairs={{1,0},{2,1},{3,2},{4,3},{5,4},{6,5},{7,6},{9,8},{10,9},{11,10},{12... | collective-permute-start | bytes 2359304 | tf_op jit(solution)/shard_map/ppermute | solution.py:19
Sparse Core Ops, SparseCore 0:
  119.7 117.1 reduce-scatter.3

commit v2 on v1

--- a/solution.py
+++ b/solution.py
@@ -81,12 +81,144 @@
     )(qkv, prev, grad)
 
 
+def bit_of(index, bit):
+    return (index // (1 << bit)) % 2
+
+
+def reduce_kernel(records, scale, *refs):
+    frames, before = refs[:records], refs[records : 2 * records]
+    own, earlier = refs[2 * records : 3 * records], refs[3 * records : 4 * records]
+    out_ref, held, landed, send_sem, recv_sem = refs[4 * records :]
+    width = frames[0].shape[1]
+    streams, blocks = lax.axis_size("stream"), lax.axis_size("tm")
+    stream, block = lax.axis_index("stream"), lax.axis_index("tm")
+    stream_bits, block_bits = streams.bit_length() - 1, blocks.bit_length() - 1
+    dims = [("stream", b, bit_of(stream, b)) for b in reversed(range(stream_bits))]
+    dims += [("tm", b, bit_of(block, b)) for b in reversed(range(block_bits))]
+    count = len(dims)
+    first = stream_bits - 1
+    rest = list(reversed(range(first))) + list(reversed(range(first + 1, count)))
+    orders = [[first] + rest[c % len(rest) :] + rest[: c % len(rest)] for c in range(3)]
+
+    def partner(d):
+        axis, b, value = dims[d]
+        return {axis: (stream if axis == "stream" else block) + (1 - 2 * value) * (1 << b)}
+
+    barrier = pltpu.get_barrier_semaphore()
+    for d in range(count):
+        pl.semaphore_signal(
+            barrier, inc=1, device_id=partner(d), device_id_type=pl.DeviceIdType.MESH
+        )
+    pl.semaphore_wait(barrier, count)
+
+    rows = width // streams
+
+    def products(parity):
+        def body(j, carry):
+            piece = 2 * j + parity
+            span = pl.ds(pl.multiple_of(piece * rows, rows), rows)
+            lead = [bit_of(piece, b) for b in reversed(range(stream_bits))]
+            for c in range(3):
+                total = 0.0
+                for r in range(records):
+                    cols = slice(c * width, (c + 1) * width)
+                    total += dot(frames[r][:, span], own[r][:, cols], TN)
+                    if c > 0:
+                        cols = slice((c - 1) * width, c * width)
+                        total += dot(before[r][:, span], earlier[r][:, cols], TN)
+                shape = held.shape[1 + stream_bits :]
+                held[(c, *lead)] = total.astype(held.dtype).reshape(shape)
+            return carry
+
+        lax.fori_loop(0, streams // 2, body, 0)
+
+    def region(c, phase, kept):
+        index = [slice(None)] * count
+        for d in orders[c][:phase]:
+            index[d] = dims[d][2]
+        last = orders[c][phase]
+        index[last] = dims[last][2] if kept else 1 - dims[last][2]
+        return (c, *index)
+
+    def copy(c, phase):
+        return pltpu.make_async_remote_copy(
+            src_ref=held.at[region(c, phase, False)],
+            dst_ref=landed.at[region(c, phase, True)],
+            send_sem=send_sem.at[c, phase],
+            recv_sem=recv_sem.at[c, phase],
+            device_id=partner(orders[c][phase]),
+            device_id_type=pl.DeviceIdType.MESH,
+        )
+
+    def merge(c, phase):
+        free = [d for d in range(count) if d not in orders[c][: phase + 1]]
+
+        def body(j, carry):
+            kept = list(region(c, phase, True))
+            arrived = list(region(c, phase, False))
+            for k, d in enumerate(free):
+                kept[1 + d] = arrived[1 + d] = bit_of(j, k)
+            kept, arrived = tuple(kept), tuple(arrived)
+            total = held[kept].astype(jnp.float32) + landed[arrived].astype(jnp.float32)
+            if free:
+                held[kept] = total.astype(held.dtype)
+            else:
+                out_ref[:, c * width : (c + 1) * width] = total * scale
+            return carry
+
+        if free:
+            lax.fori_loop(0, 1 << len(free), body, 0)
+        else:
+            body(0, 0)
+
+    products(1 - dims[first][2])
+    for c in range(3):
+        copy(c, 0).start()
+    products(dims[first][2])
+    for phase in range(count):
+        for c in range(3):
+            copy(c, phase).wait_recv()
+            merge(c, phase)
+            if phase + 1 < count:
+                copy(c, phase + 1).start()
+    for phase in range(count):
+        for c in range(3):
+            copy(c, phase).wait_send()
+
+
+def weight_gradient(frames, before, own, earlier, scale):
+    records = len(frames)
+    width = frames[0].shape[1]
+    devices = lax.axis_size("stream") * lax.axis_size("tm")
+    count = devices.bit_length() - 1
+    part = pltpu.VMEM((3, *([2] * count), width // devices, width), jnp.bfloat16)
+    operands = (*frames, *before, *own, *earlier)
+    return pl.pallas_call(
+        functools.partial(reduce_kernel, records, scale),
+        in_specs=[pl.BlockSpec(memory_space=pltpu.VMEM)] * len(operands),
+        out_specs=pl.BlockSpec(memory_space=pltpu.VMEM),
+        out_shape=jax.ShapeDtypeStruct((width // devices, 3 * width), jnp.float32),
+        scratch_shapes=[
+            part,
+            part,
+            pltpu.SemaphoreType.DMA((3, count)),
+            pltpu.SemaphoreType.DMA((3, count)),
+        ],
+        compiler_params=pltpu.CompilerParams(collective_id=0, has_side_effects=True),
+        cost_estimate=pl.CostEstimate(
+            flops=100 * records * frames[0].size * width // 10,
+            bytes_accessed=22 * records * frames[0].size,
+            transcendentals=0,
+        ),
+    )(*operands)
+
+
 def local(frames_in, w_qkv, grad_out):
     records, frame_count, width = frames_in.shape
     w_kv = w_qkv[:, width:]
     total_frames = records * frame_count * lax.axis_size("stream") * lax.axis_size("tm")
     before = [passed_along(frames_in[r], "tm", 1) for r in range(records)]
-    own_in, own, earlier, returned = [], [], [], []
+    own, earlier, returned = [], [], []
     for r in range(records):
         qkv = dot(frames_in[r], w_qkv).astype(jnp.bfloat16)
         prev = dot(before[r], w_kv).astype(jnp.bfloat16)
@@ -95,14 +227,13 @@
         returned.append(passed_along(back, "tm", -1))
         own.append(d_own)
         earlier.append(d_earlier)
-    q_terms = sum(dot(frames_in[r], own[r][:, :width], TN) for r in range(records))
-    kv_terms = sum(
-        dot(frames_in[r], own[r][:, width:], TN) + dot(before[r], earlier[r], TN)
-        for r in range(records)
-    )
-    terms = jnp.concatenate([q_terms, kv_terms], 1).astype(jnp.bfloat16)
-    reduced = lax.psum_scatter(terms, ("stream", "tm"), scatter_dimension=0, tiled=True)
-    grad_w = reduced.astype(jnp.float32) * float(total_frames) ** (-0.5)
+    grad_w = weight_gradient(
+        [frames_in[r] for r in range(records)],
+        before,
+        own,
+        earlier,
+        float(total_frames) ** (-0.5),
+    )
     grad_in = jnp.stack(
         [
             (dot(own[r], w_qkv, NT) + returned[r].astype(jnp.float32)).astype(jnp.bfloat16)

time: 247 us -> 160 us (0.65)
  waiting for transfers between devices: 99.2 us -> 10.2 us
  Pallas kernels: 31.4 us -> 95.9 us
  matrix products: 68.3 us -> 35.6 us
  between operations: 14.2 us -> 0.86 us
  local copies, waits for them, and re-layouts: 15.5 us -> 3.78 us
  other arithmetic: 4.74 us -> 1.28 us
    unnamed x2 -> x0, waiting for transfers between devices: 70.8 us -> none
    pallas_call x0 -> x1, Pallas kernels: none -> 64.4 us  [weight_gradient(): pl.pallas_call(functools.partial(reduce_kernel, records, scale), in_specs...]
    dot_general x14 -> x8, matrix products: 68.3 us -> 35.6 us  [dot(): return lax.dot_general(a, b, dims, preferred_element_type=jnp.float32)]
    ppermute x4, waiting for transfers between devices: 28.4 us -> 10.2 us  [passed_along(): lax.ppermute(value, axis, [(source, source + steps) for source in range(f...]
    unnamed x39 -> x29, local copies, waits for them, and re-layouts: 12.6 us -> 0.82 us
    concatenate x1 -> x0, other arithmetic: 3.33 us -> none  [local(): terms = jnp.concatenate([q_terms, kv_terms], 1).astype(jnp.bfloat16)]
  transfers between devices with their start and end apart: 5 -> 4, of which waited for: 4 -> 2; matrix products, arithmetic and copies ran while one was open for 16% -> 21% of each run, Pallas kernels for 6% -> 60%
where the time goes in v2:
time: 160 us
  Pallas kernels  95.9 us (60%)
  matrix products  35.6 us (22%)
  starting transfers between devices  12.2 us (8%)
  waiting for transfers between devices  10.2 us (6%)
  local copies, waits for them, and re-layouts  3.78 us (2%)
    pallas_call x1, Pallas kernels, weight_gradient(): pl.pallas_call(functools.partial(reduce_kernel, records, scale), in_specs...  64.4 us
    dot_general x8, matrix products, dot(): return lax.dot_general(a, b, dims, preferred_element_type=jnp.float32)  35.6 us
    pallas_call x2, Pallas kernels, attention(): pl.pallas_call(functools.partial(attention_kernel, width), grid=(HEADS,),...  31.5 us
    ppermute x4, starting transfers between devices, passed_along(): lax.ppermute(value, axis, [(source, source + steps) for source in range(f...  12.2 us
    ppermute x4, waiting for transfers between devices, passed_along(): lax.ppermute(value, axis, [(source, source + steps) for source in range(f...  10.2 us
  transfers between devices with their start and end apart: 4, of which 2 were waited for; matrix products, arithmetic and copies ran while one was open for 21% of the time, Pallas kernels for 60%

profile of v2, /device:TPU:0, one launch (start us, length us, event | category | flops | bytes accessed | tf_op | source)
XLA Modules:
  0.0 159.7 jit_solution(10352999275499632132)
XLA Ops:
  0.6 0.0 copy-start.1
  0.6 0.0 slice-start
  0.7 1.6 %slice_bitcast_fusion.3 = (bf16[384,1024]{1,0:T(8,128)(2,1)S(1)}, bf16[384,1024]{1,0:T(8,128)(2,1)S(1)}) fusion(bf16[2,384,1024]{2,1,0:T(8,128)(2,1)} %param.3), kind=kLoop, calls=%fused_computation.20 | loop fusion | bytes 3145728 | tf_op jit(solution)/shard_map/squeeze | solution.py:223
  2.3 0.0 copy-start.2
  2.3 0.0 copy-start.3
  2.3 5.2 %collective-permute-start = (bf16[384,1024]{1,0:T(8,128)(2,1)S(1)}, bf16[384,1024]{1,0:T(8,128)(2,1)S(1)}, u32[]{:S(2)}, u32[]{:S(2)}) collective-permute-start(bf16[384,1024]{1,0:T(8,128)(2,1)S(1)} %get-tuple-element.12.refs_0_), channel_id=1, source_target_pairs={{0,1},{1,2},{2,3},{3,4},{4,5},{5,6},{6,7},{8,9},{9,10},{10,11},{11... | collective-permute-start | bytes 2359304 | tf_op jit(solution)/shard_map/ppermute | solution.py:19
  7.5 0.0 copy-start
  7.6 0.0 slice-start.1
  7.6 3.7 %collective-permute-start.2 = (bf16[384,1024]{1,0:T(8,128)(2,1)S(1)}, bf16[384,1024]{1,0:T(8,128)(2,1)S(1)}, u32[]{:S(2)}, u32[]{:S(2)}) collective-permute-start(bf16[384,1024]{1,0:T(8,128)(2,1)S(1)} %get-tuple-element.13.refs_1_), channel_id=1, source_target_pairs={{0,1},{1,2},{2,3},{3,4},{4,5},{5,6},{6,7},{8,9},{9,10},{10,11},{11... | collective-permute-start | bytes 2359304 | tf_op jit(solution)/shard_map/ppermute | solution.py:19
  11.3 0.0 copy-done.1
  11.3 6.6 %convolution_convert_fusion.1.qkv_ref = bf16[384,3072]{1,0:T(8,128)(2,1)} fusion(bf16[1024,3072]{1,0:T(8,128)(2,1)} %param.4, bf16[2,384,1024]{2,1,0:T(8,128)(2,1)S(1)} %copy-done.1), kind=kOutput, calls=%fused_computation.1 | convolution fusion | flops 2417098752 | bytes 9437184 | tf_op jit(solution)/shard_map/dot_general | solution.py:23
  17.9 0.0 copy-done.2
  17.9 0.0 copy-done.3
  17.9 0.0 copy-done
  17.9 1.3 slice_bitcast_fusion.2
  19.2 0.0 slice-done
  19.2 0.0 slice-done.1
  19.2 3.9 %convolution_convert_fusion.qkv_ref = bf16[384,3072]{1,0:T(8,128)(2,1)} fusion(bf16[1024,3072]{1,0:T(8,128)(2,1)S(1)} %bitcast.25, bf16[2,384,1024]{2,1,0:T(8,128)(2,1)S(1)} %copy-done.1), kind=kOutput, calls=%fused_computation | convolution fusion | flops 2417098752 | bytes 9437184 | tf_op jit(solution)/shard_map/dot_general | solution.py:23
  23.1 2.3 %collective-permute-done.refs_2_ = bf16[384,1024]{1,0:T(8,128)(2,1)S(1)} collective-permute-done((bf16[384,1024]{1,0:T(8,128)(2,1)S(1)}, bf16[384,1024]{1,0:T(8,128)(2,1)S(1)}, u32[]{:S(2)}, u32[]{:S(2)}) %collective-permute-start) | collective-permute-done | bytes 786464 | tf_op jit(solution)/shard_map/ppermute | solution.py:19
  25.4 0.0 copy-start.5
  25.4 2.9 %convolution_convert_fusion.3.prev_ref = bf16[384,2048]{1,0:T(8,128)(2,1)} fusion(bf16[384,1024]{1,0:T(8,128)(2,1)S(1)} %collective-permute-done.refs_2_, bf16[1024,3072]{1,0:T(8,128)(2,1)S(1)} %bitcast.25), kind=kOutput, calls=%fused_computation.3 | convolution fusion | flops 1611399168 | bytes 6553600 | tf_op jit(solution)/shard_map/dot_general | solution.py:23
  28.3 0.0 copy-done.5
  28.3 15.7 %shard_map.50 = (bf16[384,3072]{1,0:T(8,128)(2,1)}, bf16[384,2048]{1,0:T(8,128)(2,1)}) custom-call(bf16[384,3072]{1,0:T(8,128)(2,1)} %convolution_convert_fusion.1.qkv_ref, bf16[384,2048]{1,0:T(8,128)(2,1)} %convolution_convert_fusion.3.prev_ref, bf16[384,1024]{1,0:T(8,128)(2,1)} %get-tuple-element.10.grad_ref), custom_call_target="tpu_custom_call" | custom-call | flops 3019898880 | bytes 8650752 | tf_op jit(solution)/shard_map/pallas_call | solution.py:70
  44.1 4.5 %fusion.6 = bf16[384,1024]{1,0:T(8,128)(2,1)S(1)} fusion(bf16[384,2048]{1,0:T(8,128)(2,1)} %get-tuple-element.7.refs_6_, bf16[1024,3072]{1,0:T(8,128)(2,1)} %param.4), kind=kOutput, calls=%fused_computation.13 | convolution fusion | flops 1611005952 | bytes 6553600 | tf_op jit(solution)/shard_map/dot_general | solution.py:23
  48.6 1.5 collective-permute-start.1
  50.1 0.0 collective-permute-done.2.refs_3_
  50.1 0.0 copy-start.6
  50.1 5.4 %convolution_convert_fusion.2.prev_ref = bf16[384,2048]{1,0:T(8,128)(2,1)} fusion(bf16[384,1024]{1,0:T(8,128)(2,1)S(1)} %collective-permute-done.2.refs_3_, bf16[1024,3072]{1,0:T(8,128)(2,1)} %param.4), kind=kOutput, calls=%fused_computation.2 | convolution fusion | flops 1611399168 | bytes 6553600 | tf_op jit(solution)/shard_map/dot_general | solution.py:23
  55.5 0.0 copy-done.6
  55.5 15.8 %shard_map.51 = (bf16[384,3072]{1,0:T(8,128)(2,1)}, bf16[384,2048]{1,0:T(8,128)(2,1)}) custom-call(bf16[384,3072]{1,0:T(8,128)(2,1)} %convolution_convert_fusion.qkv_ref, bf16[384,2048]{1,0:T(8,128)(2,1)} %convolution_convert_fusion.2.prev_ref, bf16[384,1024]{1,0:T(8,128)(2,1)} %get-tuple-element.11.grad_ref), custom_call_target="tpu_custom_call" | custom-call | flops 3019898880 | bytes 8650752 | tf_op jit(solution)/shard_map/pallas_call | solution.py:70
  71.3 0.0 copy-start.7
  71.3 64.4 %shard_map.52 = f32[32,3072]{1,0:T(8,128)} custom-call(bf16[384,1024]{1,0:T(8,128)(2,1)} %copy-done.2, bf16[384,1024]{1,0:T(8,128)(2,1)} %copy-done.3, bf16[384,1024]{1,0:T(8,128)(2,1)} %copy-done.5, bf16[384,1024]{1,0:T(8,128)(2,1)} %copy-done.6, bf16[384,3072]{1,0:T(8,128)(2,1)} %get-tuple-element.6.refs_4_, bf16[384,3072]{1,0:T(8,128)(2,1)} %get-tuple-element.8.refs_5_, ...), custom_call_target="tpu_custom_call" | custom-call | flops 8053063680 | bytes 17301504 | tf_op jit(solution)/shard_map/pallas_call | solution.py:196
  135.6 0.0 copy-done.7
  135.6 0.0 copy-start.8
  135.7 0.0 slice-start.2
  135.7 4.2 %fusion.9 = bf16[384,1024]{1,0:T(8,128)(2,1)S(1)} fusion(bf16[384,2048]{1,0:T(8,128)(2,1)S(1)} %copy-done.7, bf16[1024,3072]{1,0:T(8,128)(2,1)} %param.4), kind=kOutput, calls=%fused_computation.14 | convolution fusion | flops 1611005952 | bytes 6553600 | tf_op jit(solution)/shard_map/dot_general | solution.py:23
  139.8 0.0 slice-start.3
  139.8 0.0 copy-start.9
  139.9 1.8 %collective-permute-start.3 = (bf16[384,1024]{1,0:T(8,128)(2,1)S(1)}, bf16[384,1024]{1,0:T(8,128)(2,1)S(1)}, u32[]{:S(2)}, u32[]{:S(2)}) collective-permute-start(bf16[384,1024]{1,0:T(8,128)(2,1)S(1)} %fusion.9), channel_id=1, source_target_pairs={{1,0},{2,1},{3,2},{4,3},{5,4},{6,5},{7,6},{9,8},{10,9},{11,10},{12... | collective-permute-start | bytes 2359304 | tf_op jit(solution)/shard_map/ppermute | solution.py:19
  141.6 0.0 collective-permute-done.1
  141.6 0.0 copy-done.8
  141.7 5.4 %fusion.12 = bf16[1,384,1024]{2,1,0:T(8,128)(2,1)S(1)} fusion(bf16[384,1024]{1,0:T(8,128)(2,1)S(1)} %collective-permute-done.1, bf16[384,3072]{1,0:T(8,128)(2,1)S(1)} %copy-done.8, bf16[1024,3072]{1,0:T(8,128)(2,1)} %param.4), kind=kOutput, calls=%fused_computation.15 | convolution fusion | flops 2417098752 | bytes 10223616 | tf_op jit(solution)/shard_map/dot_general | solution.py:23
  147.1 7.9 %collective-permute-done.3 = bf16[384,1024]{1,0:T(8,128)(2,1)S(1)} collective-permute-done((bf16[384,1024]{1,0:T(8,128)(2,1)S(1)}, bf16[384,1024]{1,0:T(8,128)(2,1)S(1)}, u32[]{:S(2)}, u32[]{:S(2)}) %collective-permute-start.3) | collective-permute-done | bytes 786464 | tf_op jit(solution)/shard_map/ppermute | solution.py:19
  155.0 0.0 slice-done.2
  155.0 0.0 slice-done.3
  155.0 0.0 copy-done.9
  155.0 2.7 %fusion.13 = bf16[1,384,1024]{2,1,0:T(8,128)(2,1)S(1)} fusion(bf16[384,1024]{1,0:T(8,128)(2,1)S(1)} %collective-permute-done.3, bf16[384,3072]{1,0:T(8,128)(2,1)S(1)} %copy-done.9, bf16[1024,3072]{1,0:T(8,128)(2,1)S(1)} %bitcast.27), kind=kOutput, calls=%fused_computation.16 | convolution fusion | flops 2417098752 | bytes 10223616 | tf_op jit(solution)/shard_map/dot_general | solution.py:23
  157.7 0.0 copy-start.4
  157.7 1.3 pad_maximum_fusion
  159.0 0.0 copy-done.4
  159.0 0.7 copy.6
  (2 shorter events, 0.0 us)
Async XLA Ops:
  0.6 10.6 %copy-start.1 = (bf16[2,384,1024]{2,1,0:T(8,128)(2,1)S(1)}, bf16[2,384,1024]{2,1,0:T(8,128)(2,1)}, u32[]{:S(2)}) copy-start(bf16[2,384,1024]{2,1,0:T(8,128)(2,1)} %param.3) | copy-start | bytes 4718596
  0.6 18.6 %slice-start = ((s8[6291456]{0:T(1024)(128)(4,1)}), s8[4194304]{0:T(1024)(128)(4,1)S(1)}, s32[]{:S(2)}) async-start(s8[6291456]{0:T(1024)(128)(4,1)} %bitcast.24), calls=%async_computation | async-start | bytes 8388608
  2.3 15.6 %copy-start.2 = (bf16[384,1024]{1,0:T(8,128)(2,1)}, bf16[384,1024]{1,0:T(8,128)(2,1)S(1)}, u32[]{:S(2)}) copy-start(bf16[384,1024]{1,0:T(8,128)(2,1)S(1)} %get-tuple-element.12.refs_0_) | copy-start | bytes 2359300
  2.3 15.6 %copy-start.3 = (bf16[384,1024]{1,0:T(8,128)(2,1)}, bf16[384,1024]{1,0:T(8,128)(2,1)S(1)}, u32[]{:S(2)}) copy-start(bf16[384,1024]{1,0:T(8,128)(2,1)S(1)} %get-tuple-element.13.refs_1_) | copy-start | bytes 2359300
  2.3 23.1 %collective-permute-start = (bf16[384,1024]{1,0:T(8,128)(2,1)S(1)}, bf16[384,1024]{1,0:T(8,128)(2,1)S(1)}, u32[]{:S(2)}, u32[]{:S(2)}) collective-permute-start(bf16[384,1024]{1,0:T(8,128)(2,1)S(1)} %get-tuple-element.12.refs_0_), channel_id=1, source_target_pairs={{0,1},{1,2},{2,3},{3,4},{4,5},{5,6},{6,7},{8,9},{9,10},{10,11},{11... | collective-permute-start | bytes 2359304 | tf_op jit(solution)/shard_map/ppermute | solution.py:19
  7.5 10.4 %copy-start = (bf16[2,384,1024]{2,1,0:T(8,128)(2,1)S(1)}, bf16[2,384,1024]{2,1,0:T(8,128)(2,1)}, u32[]{:S(2)}) copy-start(bf16[2,384,1024]{2,1,0:T(8,128)(2,1)} %param.5) | copy-start | bytes 4718596
  7.6 11.7 %slice-start.1 = ((s8[6291456]{0:T(1024)(128)(4,1)}), s8[2097152]{0:T(1024)(128)(4,1)S(1)}, s32[]{:S(2)}) async-start(s8[6291456]{0:T(1024)(128)(4,1)} %bitcast.24), calls=%async_computation.1 | async-start | bytes 4194304
  7.6 42.5 %collective-permute-start.2 = (bf16[384,1024]{1,0:T(8,128)(2,1)S(1)}, bf16[384,1024]{1,0:T(8,128)(2,1)S(1)}, u32[]{:S(2)}, u32[]{:S(2)}) collective-permute-start(bf16[384,1024]{1,0:T(8,128)(2,1)S(1)} %get-tuple-element.13.refs_1_), channel_id=1, source_target_pairs={{0,1},{1,2},{2,3},{3,4},{4,5},{5,6},{6,7},{8,9},{9,10},{10,11},{11... | collective-permute-start | bytes 2359304 | tf_op jit(solution)/shard_map/ppermute | solution.py:19
  25.4 2.9 %copy-start.5 = (bf16[384,1024]{1,0:T(8,128)(2,1)}, bf16[384,1024]{1,0:T(8,128)(2,1)S(1)}, u32[]{:S(2)}) copy-start(bf16[384,1024]{1,0:T(8,128)(2,1)S(1)} %collective-permute-done.refs_2_) | copy-start | bytes 2359300
  48.6 93.1 %collective-permute-start.1 = (bf16[384,1024]{1,0:T(8,128)(2,1)S(1)}, bf16[384,1024]{1,0:T(8,128)(2,1)S(1)}, u32[]{:S(2)}, u32[]{:S(2)}) collective-permute-start(bf16[384,1024]{1,0:T(8,128)(2,1)S(1)} %fusion.6), channel_id=1, source_target_pairs={{1,0},{2,1},{3,2},{4,3},{5,4},{6,5},{7,6},{9,8},{10,9},{11,10},{12... | collective-permute-start | bytes 2359304 | tf_op jit(solution)/shard_map/ppermute | solution.py:19
  50.1 5.4 %copy-start.6 = (bf16[384,1024]{1,0:T(8,128)(2,1)}, bf16[384,1024]{1,0:T(8,128)(2,1)S(1)}, u32[]{:S(2)}) copy-start(bf16[384,1024]{1,0:T(8,128)(2,1)S(1)} %collective-permute-done.2.refs_3_) | copy-start | bytes 2359300
  71.3 64.4 %copy-start.7 = (bf16[384,2048]{1,0:T(8,128)(2,1)S(1)}, bf16[384,2048]{1,0:T(8,128)(2,1)}, u32[]{:S(2)}) copy-start(bf16[384,2048]{1,0:T(8,128)(2,1)} %get-tuple-element.9.refs_7_) | copy-start | bytes 4718596
  135.6 6.0 %copy-start.8 = (bf16[384,3072]{1,0:T(8,128)(2,1)S(1)}, bf16[384,3072]{1,0:T(8,128)(2,1)}, u32[]{:S(2)}) copy-start(bf16[384,3072]{1,0:T(8,128)(2,1)} %get-tuple-element.6.refs_4_) | copy-start | bytes 7077892
  135.7 19.3 %slice-start.2 = ((s8[6291456]{0:T(1024)(128)(4,1)}), s8[4194304]{0:T(1024)(128)(4,1)S(1)}, s32[]{:S(2)}) async-start(s8[6291456]{0:T(1024)(128)(4,1)} %bitcast.26), calls=%async_computation.2 | async-start | bytes 8388608
  139.8 15.2 %slice-start.3 = ((s8[6291456]{0:T(1024)(128)(4,1)}), s8[2097152]{0:T(1024)(128)(4,1)S(1)}, s32[]{:S(2)}) async-start(s8[6291456]{0:T(1024)(128)(4,1)} %bitcast.26), calls=%async_computation.3 | async-start | bytes 4194304
  139.8 15.2 %copy-start.9 = (bf16[384,3072]{1,0:T(8,128)(2,1)S(1)}, bf16[384,3072]{1,0:T(8,128)(2,1)}, u32[]{:S(2)}) copy-start(bf16[384,3072]{1,0:T(8,128)(2,1)} %get-tuple-element.8.refs_5_) | copy-start | bytes 7077892
  139.9 15.1 %collective-permute-start.3 = (bf16[384,1024]{1,0:T(8,128)(2,1)S(1)}, bf16[384,1024]{1,0:T(8,128)(2,1)S(1)}, u32[]{:S(2)}, u32[]{:S(2)}) collective-permute-start(bf16[384,1024]{1,0:T(8,128)(2,1)S(1)} %fusion.9), channel_id=1, source_target_pairs={{1,0},{2,1},{3,2},{4,3},{5,4},{6,5},{7,6},{9,8},{10,9},{11,10},{12... | collective-permute-start | bytes 2359304 | tf_op jit(solution)/shard_map/ppermute | solution.py:19
  157.7 1.3 copy-start.4

commit v3 on v2

--- a/solution.py
+++ b/solution.py
@@ -88,7 +88,9 @@
 def reduce_kernel(records, scale, *refs):
     frames, before = refs[:records], refs[records : 2 * records]
     own, earlier = refs[2 * records : 3 * records], refs[3 * records : 4 * records]
-    out_ref, held, landed, send_sem, recv_sem = refs[4 * records :]
+    returned, w_ref = refs[4 * records : 5 * records - 1], refs[5 * records - 1]
+    out_ref, grad_ref, held, landed, sums, leaving, arriving = refs[5 * records : 5 * records + 7]
+    send_sem, recv_sem, back_send_sem, back_recv_sem = refs[5 * records + 7 :]
     width = frames[0].shape[1]
     streams, blocks = lax.axis_size("stream"), lax.axis_size("tm")
     stream, block = lax.axis_index("stream"), lax.axis_index("tm")
@@ -109,7 +111,52 @@
         pl.semaphore_signal(
             barrier, inc=1, device_id=partner(d), device_id_type=pl.DeviceIdType.MESH
         )
-    pl.semaphore_wait(barrier, count)
+    has_before, has_after = block > 0, block < blocks - 1
+
+    def greet(step):
+        pl.semaphore_signal(
+            barrier,
+            inc=1,
+            device_id={"tm": block + step},
+            device_id_type=pl.DeviceIdType.MESH,
+        )
+
+    pl.when(has_before)(lambda: greet(-1))
+    pl.when(has_after)(lambda: greet(1))
+    beside = (block + blocks - 1) // blocks + (2 * blocks - 2 - block) // blocks
+    pl.semaphore_wait(barrier, count + beside)
+    back = pltpu.make_async_remote_copy(
+        src_ref=leaving,
+        dst_ref=arriving,
+        send_sem=back_send_sem,
+        recv_sem=back_recv_sem,
+        device_id={"tm": block - 1},
+        device_id_type=pl.DeviceIdType.MESH,
+    )
+
+    def by_columns(store):
+        step = 256
+
+        def body(j, carry):
+            span = pl.ds(pl.multiple_of(j * step, step), step)
+            store(span)
+            return carry
+
+        lax.fori_loop(0, width // step, body, 0)
+
+    def returning(span):
+        terms = dot(earlier[-1][...], w_ref[span, width:], NT)
+        leaving[:, span] = terms.astype(leaving.dtype)
+
+    def own_terms(r, span):
+        terms = dot(own[r][...], w_ref[span, :], NT)
+        if r < records - 1:
+            terms += returned[r][:, span].astype(jnp.float32)
+            grad_ref[r, :, span] = terms.astype(grad_ref.dtype)
+        else:
+            sums[:, span] = terms
+
+    work = [functools.partial(by_columns, functools.partial(own_terms, r)) for r in range(records)]
 
     rows = width // streams
 
@@ -171,11 +218,15 @@
         else:
             body(0, 0)
 
+    by_columns(returning)
+    pl.when(has_before)(back.start)
     products(1 - dims[first][2])
     for c in range(3):
         copy(c, 0).start()
     products(dims[first][2])
     for phase in range(count):
+        if 0 < phase <= records:
+            work[phase - 1]()
         for c in range(3):
             copy(c, phase).wait_recv()
             merge(c, phase)
@@ -184,29 +235,48 @@
     for phase in range(count):
         for c in range(3):
             copy(c, phase).wait_send()
-
-
-def weight_gradient(frames, before, own, earlier, scale):
+    pl.when(has_before)(back.wait_send)
+    last = records - 1
+
+    @pl.when(has_after)
+    def _():
+        back.wait_recv()
+        grad_ref[last] = (sums[...] + arriving[...].astype(jnp.float32)).astype(grad_ref.dtype)
+
+    @pl.when(jnp.logical_not(has_after))
+    def _():
+        grad_ref[last] = sums[...].astype(grad_ref.dtype)
+
+
+def gradients(frames, before, own, earlier, returned, w_qkv, scale):
     records = len(frames)
-    width = frames[0].shape[1]
+    rows, width = frames[0].shape
     devices = lax.axis_size("stream") * lax.axis_size("tm")
     count = devices.bit_length() - 1
     part = pltpu.VMEM((3, *([2] * count), width // devices, width), jnp.bfloat16)
-    operands = (*frames, *before, *own, *earlier)
+    operands = (*frames, *before, *own, *earlier, *returned, w_qkv)
     return pl.pallas_call(
         functools.partial(reduce_kernel, records, scale),
         in_specs=[pl.BlockSpec(memory_space=pltpu.VMEM)] * len(operands),
-        out_specs=pl.BlockSpec(memory_space=pltpu.VMEM),
-        out_shape=jax.ShapeDtypeStruct((width // devices, 3 * width), jnp.float32),
+        out_specs=[pl.BlockSpec(memory_space=pltpu.VMEM)] * 2,
+        out_shape=(
+            jax.ShapeDtypeStruct((width // devices, 3 * width), jnp.float32),
+            jax.ShapeDtypeStruct((records, rows, width), jnp.bfloat16),
+        ),
         scratch_shapes=[
             part,
             part,
+            pltpu.VMEM((rows, width), jnp.float32),
+            pltpu.VMEM((rows, width), jnp.bfloat16),
+            pltpu.VMEM((rows, width), jnp.bfloat16),
             pltpu.SemaphoreType.DMA((3, count)),
             pltpu.SemaphoreType.DMA((3, count)),
+            pltpu.SemaphoreType.DMA,
+            pltpu.SemaphoreType.DMA,
         ],
         compiler_params=pltpu.CompilerParams(collective_id=0, has_side_effects=True),
         cost_estimate=pl.CostEstimate(
-            flops=100 * records * frames[0].size * width // 10,
+            flops=20 * records * frames[0].size * width,
             bytes_accessed=22 * records * frames[0].size,
             transcendentals=0,
         ),
@@ -223,22 +293,19 @@
         qkv = dot(frames_in[r], w_qkv).astype(jnp.bfloat16)
         prev = dot(before[r], w_kv).astype(jnp.bfloat16)
         d_own, d_earlier = attention(qkv, prev, grad_out[r])
-        back = dot(d_earlier, w_kv, NT).astype(jnp.bfloat16)
-        returned.append(passed_along(back, "tm", -1))
+        if r < records - 1:
+            back = dot(d_earlier, w_kv, NT).astype(jnp.bfloat16)
+            returned.append(passed_along(back, "tm", -1))
         own.append(d_own)
         earlier.append(d_earlier)
-    grad_w = weight_gradient(
+    grad_w, grad_in = gradients(
         [frames_in[r] for r in range(records)],
         before,
         own,
         earlier,
+        returned,
+        w_qkv,
         float(total_frames) ** (-0.5),
-    )
-    grad_in = jnp.stack(
-        [
-            (dot(own[r], w_qkv, NT) + returned[r].astype(jnp.float32)).astype(jnp.bfloat16)
-            for r in range(records)
-        ]
     )
     return (grad_in, grad_w)
 

time: 160 us -> 153 us (0.956)
  matrix products: 35.6 us -> 26.3 us
  Pallas kernels: 95.9 us -> 103 us
  waiting for transfers between devices: 10.2 us -> 5.13 us
  local copies, waits for them, and re-layouts: 3.78 us -> 7.3 us
    dot_general x8 -> x5, matrix products: 35.6 us -> 26.3 us  [dot(): return lax.dot_general(a, b, dims, preferred_element_type=jnp.float32)]
    pallas_call x1, Pallas kernels: 64.4 us -> 71.2 us  [gradients(): pl.pallas_call(functools.partial(reduce_kernel, records, scale), in_specs...]
    ppermute x4 -> x3, waiting for transfers between devices: 10.2 us -> 5.13 us  [passed_along(): lax.ppermute(value, axis, [(source, source + steps) for source in range(f...]
    unnamed x29 -> x24, local copies, waits for them, and re-layouts: 0.82 us -> 4.39 us
    ppermute x4 -> x3, starting transfers between devices: 12.2 us -> 10.9 us  [passed_along(): lax.ppermute(value, axis, [(source, source + steps) for source in range(f...]
  transfers between devices with their start and end apart: 4 -> 3, of which waited for: 2 -> 1; matrix products, arithmetic and copies ran while one was open for 21% -> 18% of each run, Pallas kernels for 60% -> 21%
where the time goes in v3:
time: 153 us
  Pallas kernels  103 us (67%)
  matrix products  26.3 us (17%)
  starting transfers between devices  10.9 us (7%)
  local copies, waits for them, and re-layouts  7.3 us (5%)
  waiting for transfers between devices  5.13 us (3%)
    pallas_call x1, Pallas kernels, gradients(): pl.pallas_call(functools.partial(reduce_kernel, records, scale), in_specs...  71.2 us
    pallas_call x2, Pallas kernels, attention(): pl.pallas_call(functools.partial(attention_kernel, width), grid=(HEADS,),...  31.5 us
    dot_general x5, matrix products, dot(): return lax.dot_general(a, b, dims, preferred_element_type=jnp.float32)  26.3 us
    ppermute x3, starting transfers between devices, passed_along(): lax.ppermute(value, axis, [(source, source + steps) for source in range(f...  10.9 us
    ppermute x3, waiting for transfers between devices, passed_along(): lax.ppermute(value, axis, [(source, source + steps) for source in range(f...  5.13 us
    unnamed x24, local copies, waits for them, and re-layouts  4.39 us
  transfers between devices with their start and end apart: 3, of which 1 were waited for; matrix products, arithmetic and copies ran while one was open for 18% of the time, Pallas kernels for 21%

profile of v3, /device:TPU:0, one launch (start us, length us, event | category | flops | bytes accessed | tf_op | source)
XLA Modules:
  0.0 153.1 jit_solution(15536390575528750003)
XLA Ops:
  0.6 0.0 copy-start
  0.6 1.6 %slice_bitcast_fusion.2 = (bf16[384,1024]{1,0:T(8,128)(2,1)S(1)}, bf16[384,1024]{1,0:T(8,128)(2,1)S(1)}) fusion(bf16[2,384,1024]{2,1,0:T(8,128)(2,1)} %param.3), kind=kLoop, calls=%fused_computation.13 | loop fusion | bytes 3145728 | tf_op jit(solution)/shard_map/squeeze | solution.py:302
  2.3 0.0 copy-start.2
  2.3 0.0 copy-start.3
  2.3 0.0 copy-start.1
  2.3 5.2 %collective-permute-start = (bf16[384,1024]{1,0:T(8,128)(2,1)S(1)}, bf16[384,1024]{1,0:T(8,128)(2,1)S(1)}, u32[]{:S(2)}, u32[]{:S(2)}) collective-permute-start(bf16[384,1024]{1,0:T(8,128)(2,1)S(1)} %get-tuple-element.17.refs_0_), channel_id=1, source_target_pairs={{0,1},{1,2},{2,3},{3,4},{4,5},{5,6},{6,7},{8,9},{9,10},{10,11},{11... | collective-permute-start | bytes 2359304 | tf_op jit(solution)/shard_map/ppermute | solution.py:19
  7.5 4.3 %collective-permute-start.1 = (bf16[384,1024]{1,0:T(8,128)(2,1)S(1)}, bf16[384,1024]{1,0:T(8,128)(2,1)}, u32[]{:S(2)}, u32[]{:S(2)}) collective-permute-start(bf16[384,1024]{1,0:T(8,128)(2,1)S(1)} %get-tuple-element.16.refs_1_), channel_id=1, source_target_pairs={{0,1},{1,2},{2,3},{3,4},{4,5},{5,6},{6,7},{8,9},{9,10},{10,11},{11... | collective-permute-start | bytes 2359304 | tf_op jit(solution)/shard_map/ppermute | solution.py:19
  11.8 0.0 copy-done
  11.8 0.0 slice-start
  11.8 1.3 slice_bitcast_fusion
  13.1 0.0 copy-done.1
  13.1 0.0 slice-start.1
  13.1 7.1 %convolution_convert_fusion.1.qkv_ref = bf16[384,3072]{1,0:T(8,128)(2,1)} fusion(bf16[1024,3072]{1,0:T(8,128)(2,1)} %refs_9_.1, bf16[2,384,1024]{2,1,0:T(8,128)(2,1)S(1)} %copy-done.1), kind=kOutput, calls=%fused_computation.1 | convolution fusion | flops 2417098752 | bytes 9437184 | tf_op jit(solution)/shard_map/dot_general | solution.py:23
  20.2 0.0 copy-done.2
  20.2 0.0 copy-done.3
  20.2 5.1 %collective-permute-done.refs_2_ = bf16[384,1024]{1,0:T(8,128)(2,1)S(1)} collective-permute-done((bf16[384,1024]{1,0:T(8,128)(2,1)S(1)}, bf16[384,1024]{1,0:T(8,128)(2,1)S(1)}, u32[]{:S(2)}, u32[]{:S(2)}) %collective-permute-start) | collective-permute-done | bytes 786464 | tf_op jit(solution)/shard_map/ppermute | solution.py:19
  25.4 0.0 slice-done
  25.4 0.0 slice-done.1
  25.4 0.0 copy-start.5
  25.4 2.9 %fusion.6.prev_ref = bf16[384,2048]{1,0:T(8,128)(2,1)} fusion(bf16[384,1024]{1,0:T(8,128)(2,1)S(1)} %collective-permute-done.refs_2_, bf16[1024,3072]{1,0:T(8,128)(2,1)S(1)} %bitcast.16), kind=kOutput, calls=%fused_computation.8 | convolution fusion | flops 1611399168 | bytes 6553600 | tf_op jit(solution)/shard_map/dot_general | solution.py:23
  28.3 0.0 copy-done.5
  28.3 15.7 %shard_map.50 = (bf16[384,3072]{1,0:T(8,128)(2,1)}, bf16[384,2048]{1,0:T(8,128)(2,1)}) custom-call(bf16[384,3072]{1,0:T(8,128)(2,1)} %convolution_convert_fusion.1.qkv_ref, bf16[384,2048]{1,0:T(8,128)(2,1)} %fusion.6.prev_ref, bf16[384,1024]{1,0:T(8,128)(2,1)} %get-tuple-element.15.grad_ref), custom_call_target="tpu_custom_call" | custom-call | flops 3019898880 | bytes 8650752 | tf_op jit(solution)/shard_map/pallas_call | solution.py:70
  44.0 0.0 slice-start.2
  44.0 5.5 %fusion.12 = bf16[384,1024]{1,0:T(8,128)(2,1)} fusion(bf16[384,2048]{1,0:T(8,128)(2,1)} %get-tuple-element.10.refs_6_, bf16[1024,3072]{1,0:T(8,128)(2,1)} %refs_9_.1), kind=kOutput, calls=%fused_computation.10 | convolution fusion | flops 1611005952 | bytes 6553600 | tf_op jit(solution)/shard_map/dot_general | solution.py:23
  49.6 0.0 slice-start.3
  49.6 1.4 collective-permute-start.2
  51.0 6.7 %convolution_convert_fusion.qkv_ref = bf16[384,3072]{1,0:T(8,128)(2,1)} fusion(bf16[1024,3072]{1,0:T(8,128)(2,1)} %refs_9_.1, bf16[2,384,1024]{2,1,0:T(8,128)(2,1)S(1)} %copy-done.1), kind=kOutput, calls=%fused_computation | convolution fusion | flops 2417098752 | bytes 9437184 | tf_op jit(solution)/shard_map/dot_general | solution.py:23
  57.6 0.0 collective-permute-done.1.refs_3_
  57.6 0.0 slice-done.2
  57.6 0.0 slice-done.3
  57.7 4.1 %fusion.9.prev_ref = bf16[384,2048]{1,0:T(8,128)(2,1)} fusion(bf16[384,1024]{1,0:T(8,128)(2,1)} %collective-permute-done.1.refs_3_, bf16[1024,3072]{1,0:T(8,128)(2,1)S(1)} %bitcast.18), kind=kOutput, calls=%fused_computation.9 | convolution fusion | flops 1611399168 | bytes 6553600 | tf_op jit(solution)/shard_map/dot_general | solution.py:23
  61.7 15.8 %shard_map.51 = (bf16[384,3072]{1,0:T(8,128)(2,1)}, bf16[384,2048]{1,0:T(8,128)(2,1)}) custom-call(bf16[384,3072]{1,0:T(8,128)(2,1)} %convolution_convert_fusion.qkv_ref, bf16[384,2048]{1,0:T(8,128)(2,1)} %fusion.9.prev_ref, bf16[384,1024]{1,0:T(8,128)(2,1)} %get-tuple-element.14.grad_ref), custom_call_target="tpu_custom_call" | custom-call | flops 3019898880 | bytes 8650752 | tf_op jit(solution)/shard_map/pallas_call | solution.py:70
  77.5 0.0 collective-permute-done.2.refs_8_
  77.5 0.0 copy-start.6
  77.5 0.9 copy-done.6
  78.4 71.2 %shard_map.52 = (f32[32,3072]{1,0:T(8,128)}, bf16[2,384,1024]{2,1,0:T(8,128)(2,1)}) custom-call(bf16[384,1024]{1,0:T(8,128)(2,1)} %copy-done.3, bf16[384,1024]{1,0:T(8,128)(2,1)} %copy-done.2, bf16[384,1024]{1,0:T(8,128)(2,1)} %copy-done.5, bf16[384,1024]{1,0:T(8,128)(2,1)} %collective-permute-done.1.refs_3_, bf16[384,3072]{1,0:T(8,128)(2,1)} %get-tuple-element.8.refs_4_, ...), custom_call_target="tpu_custom_call" | custom-call | flops 16106127360 | bytes 17301504 | tf_op jit(solution)/shard_map/pallas_call | solution.py:258
  149.6 0.0 copy-start.4
  149.7 2.7 %copy.7 = bf16[2,384,1024]{2,1,0:T(8,128)(2,1)} copy(bf16[2,384,1024]{2,1,0:T(8,128)(2,1)} %get-tuple-element.20) | data formatting | bytes 3145728
  152.4 0.0 copy-done.4
  152.4 0.7 copy.8
  (2 shorter events, 0.0 us)
Async XLA Ops:
  0.6 11.2 %copy-start = (bf16[2,384,1024]{2,1,0:T(8,128)(2,1)S(1)}, bf16[2,384,1024]{2,1,0:T(8,128)(2,1)}, u32[]{:S(2)}) copy-start(bf16[2,384,1024]{2,1,0:T(8,128)(2,1)} %param.5) | copy-start | bytes 4718596
  2.3 18.0 %copy-start.2 = (bf16[384,1024]{1,0:T(8,128)(2,1)}, bf16[384,1024]{1,0:T(8,128)(2,1)S(1)}, u32[]{:S(2)}) copy-start(bf16[384,1024]{1,0:T(8,128)(2,1)S(1)} %get-tuple-element.16.refs_1_) | copy-start | bytes 2359300
  2.3 18.0 %copy-start.3 = (bf16[384,1024]{1,0:T(8,128)(2,1)}, bf16[384,1024]{1,0:T(8,128)(2,1)S(1)}, u32[]{:S(2)}) copy-start(bf16[384,1024]{1,0:T(8,128)(2,1)S(1)} %get-tuple-element.17.refs_0_) | copy-start | bytes 2359300
  2.3 10.8 %copy-start.1 = (bf16[2,384,1024]{2,1,0:T(8,128)(2,1)S(1)}, bf16[2,384,1024]{2,1,0:T(8,128)(2,1)}, u32[]{:S(2)}) copy-start(bf16[2,384,1024]{2,1,0:T(8,128)(2,1)} %param.3) | copy-start | bytes 4718596
  2.3 23.1 %collective-permute-start = (bf16[384,1024]{1,0:T(8,128)(2,1)S(1)}, bf16[384,1024]{1,0:T(8,128)(2,1)S(1)}, u32[]{:S(2)}, u32[]{:S(2)}) collective-permute-start(bf16[384,1024]{1,0:T(8,128)(2,1)S(1)} %get-tuple-element.17.refs_0_), channel_id=1, source_target_pairs={{0,1},{1,2},{2,3},{3,4},{4,5},{5,6},{6,7},{8,9},{9,10},{10,11},{11... | collective-permute-start | bytes 2359304 | tf_op jit(solution)/shard_map/ppermute | solution.py:19
  7.5 50.1 %collective-permute-start.1 = (bf16[384,1024]{1,0:T(8,128)(2,1)S(1)}, bf16[384,1024]{1,0:T(8,128)(2,1)}, u32[]{:S(2)}, u32[]{:S(2)}) collective-permute-start(bf16[384,1024]{1,0:T(8,128)(2,1)S(1)} %get-tuple-element.16.refs_1_), channel_id=1, source_target_pairs={{0,1},{1,2},{2,3},{3,4},{4,5},{5,6},{6,7},{8,9},{9,10},{10,11},{11... | collective-permute-start | bytes 2359304 | tf_op jit(solution)/shard_map/ppermute | solution.py:19
  11.8 13.6 %slice-start = ((s8[6291456]{0:T(1024)(128)(4,1)}), s8[4194304]{0:T(1024)(128)(4,1)S(1)}, s32[]{:S(2)}) async-start(s8[6291456]{0:T(1024)(128)(4,1)} %bitcast.15), calls=%async_computation | async-start | bytes 8388608
  13.1 12.3 %slice-start.1 = ((s8[6291456]{0:T(1024)(128)(4,1)}), s8[2097152]{0:T(1024)(128)(4,1)S(1)}, s32[]{:S(2)}) async-start(s8[6291456]{0:T(1024)(128)(4,1)} %bitcast.15), calls=%async_computation.1 | async-start | bytes 4194304
  25.4 2.9 %copy-start.5 = (bf16[384,1024]{1,0:T(8,128)(2,1)}, bf16[384,1024]{1,0:T(8,128)(2,1)S(1)}, u32[]{:S(2)}) copy-start(bf16[384,1024]{1,0:T(8,128)(2,1)S(1)} %collective-permute-done.refs_2_) | copy-start | bytes 2359300
  44.0 13.6 %slice-start.2 = ((s8[6291456]{0:T(1024)(128)(4,1)}), s8[4194304]{0:T(1024)(128)(4,1)S(1)}, s32[]{:S(2)}) async-start(s8[6291456]{0:T(1024)(128)(4,1)} %bitcast.17), calls=%async_computation.2 | async-start | bytes 8388608
  49.6 8.1 %slice-start.3 = ((s8[6291456]{0:T(1024)(128)(4,1)}), s8[2097152]{0:T(1024)(128)(4,1)S(1)}, s32[]{:S(2)}) async-start(s8[6291456]{0:T(1024)(128)(4,1)} %bitcast.17), calls=%async_computation.3 | async-start | bytes 4194304
  49.6 27.9 %collective-permute-start.2 = (bf16[384,1024]{1,0:T(8,128)(2,1)}, bf16[384,1024]{1,0:T(8,128)(2,1)S(1)}, u32[]{:S(2)}, u32[]{:S(2)}) collective-permute-start(bf16[384,1024]{1,0:T(8,128)(2,1)} %fusion.12), channel_id=1, source_target_pairs={{1,0},{2,1},{3,2},{4,3},{5,4},{6,5},{7,6},{9,8},{10,9},{11,10},{12... | collective-permute-start | bytes 2359304 | tf_op jit(solution)/shard_map/ppermute | solution.py:19
  77.5 0.9 copy-start.6
  149.6 2.7 %copy-start.4 = (f32[32,3072]{1,0:T(8,128)S(1)}, f32[32,3072]{1,0:T(8,128)}, u32[]{:S(2)}) copy-start(f32[32,3072]{1,0:T(8,128)} %get-tuple-element.21) | copy-start | bytes 1179652

commit v4 on v3

--- a/solution.py
+++ b/solution.py
@@ -8,6 +8,7 @@
 from jax.sharding import PartitionSpec as P
 
 HEADS = 8
+TOGETHER = 2
 LOG2E = 1.4426950408889634
 NT = (((1,), (1,)), ((), ()))
 TN = (((0,), (0,)), ((), ()))
@@ -28,36 +29,40 @@
     scale = head_size ** (-0.5)
     bias = jnp.where(lax.axis_index("tm") > 0, 0.0, -1e30).astype(jnp.float32)
 
-    def columns(section):
-        start = section * width + pl.program_id(0) * head_size
-        return pl.ds(pl.multiple_of(start, head_size), head_size)
-
-    q = qkv_ref[:, columns(0)]
-    k_own = qkv_ref[:, columns(1)]
-    v_own = qkv_ref[:, columns(2)]
-    k_prev = prev_ref[:, columns(0)]
-    v_prev = prev_ref[:, columns(1)]
-    grad = grad_ref[:, columns(0)]
-    s_own = dot(k_own, q, NT)
-    s_prev = dot(k_prev, q, NT) + bias
-    peak = jnp.maximum(jnp.max(s_own, 0, keepdims=True), jnp.max(s_prev, 0, keepdims=True))
-    e_own = jnp.exp2((s_own - peak) * (scale * LOG2E))
-    e_prev = jnp.exp2((s_prev - peak) * (scale * LOG2E))
-    total = jnp.sum(e_own, 0, keepdims=True) + jnp.sum(e_prev, 0, keepdims=True)
-    inverse = 1.0 / total
-    p_own = e_own * inverse
-    p_prev = e_prev * inverse
-    dp_own = dot(v_own, grad, NT)
-    dp_prev = dot(v_prev, grad, NT)
-    delta = jnp.sum(p_own * dp_own, 0, keepdims=True) + jnp.sum(p_prev * dp_prev, 0, keepdims=True)
-    ds_own = (p_own * (dp_own - delta)).astype(jnp.bfloat16)
-    ds_prev = (p_prev * (dp_prev - delta)).astype(jnp.bfloat16)
-    dq = dot(ds_own, k_own, TN) + dot(ds_prev, k_prev, TN)
-    own_ref[:, columns(0)] = (dq * scale).astype(jnp.bfloat16)
-    own_ref[:, columns(1)] = (dot(ds_own, q) * scale).astype(jnp.bfloat16)
-    own_ref[:, columns(2)] = dot(p_own.astype(jnp.bfloat16), grad).astype(jnp.bfloat16)
-    earlier_ref[:, columns(0)] = (dot(ds_prev, q) * scale).astype(jnp.bfloat16)
-    earlier_ref[:, columns(1)] = dot(p_prev.astype(jnp.bfloat16), grad).astype(jnp.bfloat16)
+    def one_head(turn):
+        def columns(section):
+            start = section * width + (pl.program_id(0) * TOGETHER + turn) * head_size
+            return pl.ds(pl.multiple_of(start, head_size), head_size)
+
+        q = qkv_ref[:, columns(0)]
+        k_own = qkv_ref[:, columns(1)]
+        v_own = qkv_ref[:, columns(2)]
+        k_prev = prev_ref[:, columns(0)]
+        v_prev = prev_ref[:, columns(1)]
+        grad = grad_ref[:, columns(0)]
+        s_own = dot(k_own, q, NT)
+        s_prev = dot(k_prev, q, NT) + bias
+        peak = jnp.maximum(jnp.max(s_own, 0, keepdims=True), jnp.max(s_prev, 0, keepdims=True))
+        e_own = jnp.exp2((s_own - peak) * (scale * LOG2E))
+        e_prev = jnp.exp2((s_prev - peak) * (scale * LOG2E))
+        total = jnp.sum(e_own, 0, keepdims=True) + jnp.sum(e_prev, 0, keepdims=True)
+        inverse = 1.0 / total
+        p_own = e_own * inverse
+        p_prev = e_prev * inverse
+        dp_own = dot(v_own, grad, NT)
+        dp_prev = dot(v_prev, grad, NT)
+        delta = jnp.sum(p_own * dp_own, 0, keepdims=True) + jnp.sum(p_prev * dp_prev, 0, keepdims=True)
+        ds_own = (p_own * (dp_own - delta)).astype(jnp.bfloat16)
+        ds_prev = (p_prev * (dp_prev - delta)).astype(jnp.bfloat16)
+        dq = dot(ds_own, k_own, TN) + dot(ds_prev, k_prev, TN)
+        own_ref[:, columns(0)] = (dq * scale).astype(jnp.bfloat16)
+        own_ref[:, columns(1)] = (dot(ds_own, q) * scale).astype(jnp.bfloat16)
+        own_ref[:, columns(2)] = dot(p_own.astype(jnp.bfloat16), grad).astype(jnp.bfloat16)
+        earlier_ref[:, columns(0)] = (dot(ds_prev, q) * scale).astype(jnp.bfloat16)
+        earlier_ref[:, columns(1)] = dot(p_prev.astype(jnp.bfloat16), grad).astype(jnp.bfloat16)
+
+    for turn in range(TOGETHER):
+        one_head(turn)
 
 
 def attention(qkv, prev, grad):
@@ -69,7 +74,7 @@
     )
     return pl.pallas_call(
         functools.partial(attention_kernel, width),
-        grid=(HEADS,),
+        grid=(HEADS // TOGETHER,),
         in_specs=[whole(qkv), whole(prev), whole(grad)],
         out_specs=[whole(o) for o in outs],
         out_shape=outs,
@@ -289,10 +294,11 @@
     total_frames = records * frame_count * lax.axis_size("stream") * lax.axis_size("tm")
     before = [passed_along(frames_in[r], "tm", 1) for r in range(records)]
     own, earlier, returned = [], [], []
+    joined = [dot(frames_in[r], w_qkv).astype(jnp.bfloat16) for r in range(records)]
+    before[0], *joined = lax.optimization_barrier((before[0], *joined))
     for r in range(records):
-        qkv = dot(frames_in[r], w_qkv).astype(jnp.bfloat16)
         prev = dot(before[r], w_kv).astype(jnp.bfloat16)
-        d_own, d_earlier = attention(qkv, prev, grad_out[r])
+        d_own, d_earlier = attention(joined[r], prev, grad_out[r])
         if r < records - 1:
             back = dot(d_earlier, w_kv, NT).astype(jnp.bfloat16)
             returned.append(passed_along(back, "tm", -1))

time: 153 us -> 145 us (0.948)
  waiting for transfers between devices: 5.13 us -> 1.49 us
  matrix products: 26.3 us -> 23.1 us
  Pallas kernels: 103 us -> 101 us
    ppermute x3, waiting for transfers between devices: 5.13 us -> 1.49 us  [passed_along(): lax.ppermute(value, axis, [(source, source + steps) for source in range(f...]
    dot_general x5, matrix products: 26.3 us -> 23.1 us  [dot(): return lax.dot_general(a, b, dims, preferred_element_type=jnp.float32)]
    pallas_call x2, Pallas kernels: 31.5 us -> 29.9 us  [attention(): pl.pallas_call(functools.partial(attention_kernel, width), grid=(HEADS //...]
    unnamed x24 -> x22, local copies, waits for them, and re-layouts: 4.39 us -> 3.51 us
  transfers between devices with their start and end apart: 3 -> 3, of which waited for: 1 -> 1; matrix products, arithmetic and copies ran while one was open for 18% -> 17% of each run, Pallas kernels for 21% -> 21%
where the time goes in v4:
time: 145 us; the launch traced here: 144 us
  Pallas kernels  101 us (70%)
  matrix products  23.1 us (16%)
  starting transfers between devices  11.2 us (8%)
  local copies, waits for them, and re-layouts  6.41 us (4%)
  waiting for transfers between devices  1.49 us (1%)
    pallas_call x1, Pallas kernels, gradients(): pl.pallas_call(functools.partial(reduce_kernel, records, scale), in_specs...  71.5 us
    pallas_call x2, Pallas kernels, attention(): pl.pallas_call(functools.partial(attention_kernel, width), grid=(HEADS //...  29.9 us
    dot_general x5, matrix products, dot(): return lax.dot_general(a, b, dims, preferred_element_type=jnp.float32)  23.1 us
    ppermute x3, starting transfers between devices, passed_along(): lax.ppermute(value, axis, [(source, source + steps) for source in range(f...  11.2 us
    unnamed x22, local copies, waits for them, and re-layouts  3.51 us
  transfers between devices with their start and end apart: 3, of which 1 were waited for; matrix products, arithmetic and copies ran while one was open for 17% of the time, Pallas kernels for 21%

profile of v4, /device:TPU:0, one launch (start us, length us, event | category | flops | bytes accessed | tf_op | source)
XLA Modules:
  0.0 144.3 jit_solution(17452640464521122924)
XLA Ops:
  0.6 0.0 copy-start.1
  0.6 0.0 slice-start
  0.7 1.6 %slice_bitcast_fusion.2 = (bf16[384,1024]{1,0:T(8,128)(2,1)S(1)}, bf16[384,1024]{1,0:T(8,128)(2,1)S(1)}) fusion(bf16[2,384,1024]{2,1,0:T(8,128)(2,1)} %param.3), kind=kLoop, calls=%fused_computation.13 | loop fusion | bytes 3145728 | tf_op jit(solution)/shard_map/squeeze | solution.py:308
  2.3 0.0 copy-start.2
  2.3 0.0 copy-start.3
  2.3 5.2 %collective-permute-start = (bf16[384,1024]{1,0:T(8,128)(2,1)S(1)}, bf16[384,1024]{1,0:T(8,128)(2,1)S(1)}, u32[]{:S(2)}, u32[]{:S(2)}) collective-permute-start(bf16[384,1024]{1,0:T(8,128)(2,1)S(1)} %get-tuple-element.23.refs_0_), channel_id=1, source_target_pairs={{0,1},{1,2},{2,3},{3,4},{4,5},{5,6},{6,7},{8,9},{9,10},{10,11},{11... | collective-permute-start | bytes 2359304 | tf_op jit(solution)/shard_map/ppermute | solution.py:20
  7.5 0.0 copy-start
  7.6 0.0 slice-start.1
  7.6 4.5 %collective-permute-start.1 = (bf16[384,1024]{1,0:T(8,128)(2,1)S(1)}, bf16[384,1024]{1,0:T(8,128)(2,1)}, u32[]{:S(2)}, u32[]{:S(2)}) collective-permute-start(bf16[384,1024]{1,0:T(8,128)(2,1)S(1)} %get-tuple-element.22.refs_1_), channel_id=1, source_target_pairs={{0,1},{1,2},{2,3},{3,4},{4,5},{5,6},{6,7},{8,9},{9,10},{10,11},{11... | collective-permute-start | bytes 2359304 | tf_op jit(solution)/shard_map/ppermute | solution.py:20
  12.1 0.0 copy-done.1
  12.1 6.6 %convolution_convert_fusion.1.qkv_ref = bf16[384,3072]{1,0:T(8,128)(2,1)} fusion(bf16[1024,3072]{1,0:T(8,128)(2,1)} %refs_9_.1, bf16[2,384,1024]{2,1,0:T(8,128)(2,1)S(1)} %copy-done.1), kind=kOutput, calls=%fused_computation.1 | convolution fusion | flops 2417098752 | bytes 9437184 | tf_op jit(solution)/shard_map/dot_general | solution.py:24
  18.7 0.0 copy-done.2
  18.7 0.0 copy-done.3
  18.7 0.0 copy-done
  18.7 1.3 slice_bitcast_fusion
  20.0 0.0 slice-done
  20.0 0.0 slice-done.1
  20.0 3.9 %convolution_convert_fusion.qkv_ref = bf16[384,3072]{1,0:T(8,128)(2,1)} fusion(bf16[1024,3072]{1,0:T(8,128)(2,1)S(1)} %bitcast.16, bf16[2,384,1024]{2,1,0:T(8,128)(2,1)S(1)} %copy-done.1), kind=kOutput, calls=%fused_computation | convolution fusion | flops 2417098752 | bytes 9437184 | tf_op jit(solution)/shard_map/dot_general | solution.py:24
  23.9 1.5 %collective-permute-done.refs_2_ = bf16[384,1024]{1,0:T(8,128)(2,1)S(1)} collective-permute-done((bf16[384,1024]{1,0:T(8,128)(2,1)S(1)}, bf16[384,1024]{1,0:T(8,128)(2,1)S(1)}, u32[]{:S(2)}, u32[]{:S(2)}) %collective-permute-start) | collective-permute-done | bytes 786464 | tf_op jit(solution)/shard_map/ppermute | solution.py:20
  25.4 0.0 copy-start.5
  25.4 2.9 %fusion.6.prev_ref = bf16[384,2048]{1,0:T(8,128)(2,1)} fusion(bf16[384,1024]{1,0:T(8,128)(2,1)S(1)} %collective-permute-done.refs_2_, bf16[1024,3072]{1,0:T(8,128)(2,1)S(1)} %bitcast.16), kind=kOutput, calls=%fused_computation.8 | convolution fusion | flops 1611399168 | bytes 6553600 | tf_op jit(solution)/shard_map/dot_general | solution.py:24
  28.3 0.0 copy-done.5
  28.3 0.0 slice-start.2
  28.3 15.0 %shard_map.50 = (bf16[384,3072]{1,0:T(8,128)(2,1)}, bf16[384,2048]{1,0:T(8,128)(2,1)}) custom-call(bf16[384,3072]{1,0:T(8,128)(2,1)} %convolution_convert_fusion.1.qkv_ref, bf16[384,2048]{1,0:T(8,128)(2,1)} %fusion.6.prev_ref, bf16[384,1024]{1,0:T(8,128)(2,1)} %get-tuple-element.21.grad_ref), custom_call_target="tpu_custom_call" | custom-call | flops 3019898880 | bytes 8650752 | tf_op jit(solution)/shard_map/pallas_call | solution.py:75
  43.3 0.0 slice-start.3
  43.3 5.5 %fusion.12 = bf16[384,1024]{1,0:T(8,128)(2,1)} fusion(bf16[384,2048]{1,0:T(8,128)(2,1)} %get-tuple-element.16.refs_6_, bf16[1024,3072]{1,0:T(8,128)(2,1)} %refs_9_.1), kind=kOutput, calls=%fused_computation.10 | convolution fusion | flops 1611005952 | bytes 6553600 | tf_op jit(solution)/shard_map/dot_general | solution.py:24
  48.9 1.5 %collective-permute-start.2 = (bf16[384,1024]{1,0:T(8,128)(2,1)}, bf16[384,1024]{1,0:T(8,128)(2,1)}, u32[]{:S(2)}, u32[]{:S(2)}) collective-permute-start(bf16[384,1024]{1,0:T(8,128)(2,1)} %fusion.12), channel_id=1, source_target_pairs={{1,0},{2,1},{3,2},{4,3},{5,4},{6,5},{7,6},{9,8},{10,9},{11,10},{12... | collective-permute-start | bytes 2359304 | tf_op jit(solution)/shard_map/ppermute | solution.py:20
  50.3 0.0 collective-permute-done.1.refs_3_
  50.3 0.0 slice-done.2
  50.4 0.0 slice-done.3
  50.4 4.1 %fusion.9.prev_ref = bf16[384,2048]{1,0:T(8,128)(2,1)} fusion(bf16[384,1024]{1,0:T(8,128)(2,1)} %collective-permute-done.1.refs_3_, bf16[1024,3072]{1,0:T(8,128)(2,1)S(1)} %bitcast.18), kind=kOutput, calls=%fused_computation.9 | convolution fusion | flops 1611399168 | bytes 6553600 | tf_op jit(solution)/shard_map/dot_general | solution.py:24
  54.4 14.9 %shard_map.51 = (bf16[384,3072]{1,0:T(8,128)(2,1)}, bf16[384,2048]{1,0:T(8,128)(2,1)}) custom-call(bf16[384,3072]{1,0:T(8,128)(2,1)} %convolution_convert_fusion.qkv_ref, bf16[384,2048]{1,0:T(8,128)(2,1)} %fusion.9.prev_ref, bf16[384,1024]{1,0:T(8,128)(2,1)} %get-tuple-element.20.grad_ref), custom_call_target="tpu_custom_call" | custom-call | flops 3019898880 | bytes 8650752 | tf_op jit(solution)/shard_map/pallas_call | solution.py:75
  69.3 0.0 collective-permute-done.2.refs_8_
  69.3 71.5 %shard_map.52 = (f32[32,3072]{1,0:T(8,128)}, bf16[2,384,1024]{2,1,0:T(8,128)(2,1)}) custom-call(bf16[384,1024]{1,0:T(8,128)(2,1)} %copy-done.3, bf16[384,1024]{1,0:T(8,128)(2,1)} %copy-done.2, bf16[384,1024]{1,0:T(8,128)(2,1)} %copy-done.5, bf16[384,1024]{1,0:T(8,128)(2,1)} %collective-permute-done.1.refs_3_, bf16[384,3072]{1,0:T(8,128)(2,1)} %get-tuple-element.13.refs_4_, ...), custom_call_target="tpu_custom_call" | custom-call | flops 16106127360 | bytes 17301504 | tf_op jit(solution)/shard_map/pallas_call | solution.py:263
  140.9 0.0 copy-start.4
  140.9 2.7 %copy.7 = bf16[2,384,1024]{2,1,0:T(8,128)(2,1)} copy(bf16[2,384,1024]{2,1,0:T(8,128)(2,1)} %get-tuple-element.26) | data formatting | bytes 3145728
  143.6 0.0 copy-done.4
  143.6 0.7 copy.8
  (2 shorter events, 0.0 us)
Async XLA Ops:
  0.6 11.5 %copy-start.1 = (bf16[2,384,1024]{2,1,0:T(8,128)(2,1)S(1)}, bf16[2,384,1024]{2,1,0:T(8,128)(2,1)}, u32[]{:S(2)}) copy-start(bf16[2,384,1024]{2,1,0:T(8,128)(2,1)} %param.3) | copy-start | bytes 4718596
  0.6 19.4 %slice-start = ((s8[6291456]{0:T(1024)(128)(4,1)}), s8[4194304]{0:T(1024)(128)(4,1)S(1)}, s32[]{:S(2)}) async-start(s8[6291456]{0:T(1024)(128)(4,1)} %bitcast.15), calls=%async_computation | async-start | bytes 8388608
  2.3 16.4 %copy-start.2 = (bf16[384,1024]{1,0:T(8,128)(2,1)}, bf16[384,1024]{1,0:T(8,128)(2,1)S(1)}, u32[]{:S(2)}) copy-start(bf16[384,1024]{1,0:T(8,128)(2,1)S(1)} %get-tuple-element.22.refs_1_) | copy-start | bytes 2359300
  2.3 16.4 %copy-start.3 = (bf16[384,1024]{1,0:T(8,128)(2,1)}, bf16[384,1024]{1,0:T(8,128)(2,1)S(1)}, u32[]{:S(2)}) copy-start(bf16[384,1024]{1,0:T(8,128)(2,1)S(1)} %get-tuple-element.23.refs_0_) | copy-start | bytes 2359300
  2.3 23.1 %collective-permute-start = (bf16[384,1024]{1,0:T(8,128)(2,1)S(1)}, bf16[384,1024]{1,0:T(8,128)(2,1)S(1)}, u32[]{:S(2)}, u32[]{:S(2)}) collective-permute-start(bf16[384,1024]{1,0:T(8,128)(2,1)S(1)} %get-tuple-element.23.refs_0_), channel_id=1, source_target_pairs={{0,1},{1,2},{2,3},{3,4},{4,5},{5,6},{6,7},{8,9},{9,10},{10,11},{11... | collective-permute-start | bytes 2359304 | tf_op jit(solution)/shard_map/ppermute | solution.py:20
  7.5 11.2 %copy-start = (bf16[2,384,1024]{2,1,0:T(8,128)(2,1)S(1)}, bf16[2,384,1024]{2,1,0:T(8,128)(2,1)}, u32[]{:S(2)}) copy-start(bf16[2,384,1024]{2,1,0:T(8,128)(2,1)} %param.5) | copy-start | bytes 4718596
  7.6 12.4 %slice-start.1 = ((s8[6291456]{0:T(1024)(128)(4,1)}), s8[2097152]{0:T(1024)(128)(4,1)S(1)}, s32[]{:S(2)}) async-start(s8[6291456]{0:T(1024)(128)(4,1)} %bitcast.15), calls=%async_computation.1 | async-start | bytes 4194304
  7.6 42.8 %collective-permute-start.1 = (bf16[384,1024]{1,0:T(8,128)(2,1)S(1)}, bf16[384,1024]{1,0:T(8,128)(2,1)}, u32[]{:S(2)}, u32[]{:S(2)}) collective-permute-start(bf16[384,1024]{1,0:T(8,128)(2,1)S(1)} %get-tuple-element.22.refs_1_), channel_id=1, source_target_pairs={{0,1},{1,2},{2,3},{3,4},{4,5},{5,6},{6,7},{8,9},{9,10},{10,11},{11... | collective-permute-start | bytes 2359304 | tf_op jit(solution)/shard_map/ppermute | solution.py:20
  25.4 2.9 %copy-start.5 = (bf16[384,1024]{1,0:T(8,128)(2,1)}, bf16[384,1024]{1,0:T(8,128)(2,1)S(1)}, u32[]{:S(2)}) copy-start(bf16[384,1024]{1,0:T(8,128)(2,1)S(1)} %collective-permute-done.refs_2_) | copy-start | bytes 2359300
  28.3 22.0 %slice-start.2 = ((s8[6291456]{0:T(1024)(128)(4,1)}), s8[2097152]{0:T(1024)(128)(4,1)S(1)}, s32[]{:S(2)}) async-start(s8[6291456]{0:T(1024)(128)(4,1)} %bitcast.17), calls=%async_computation.2 | async-start | bytes 4194304
  43.3 7.0 %slice-start.3 = ((s8[6291456]{0:T(1024)(128)(4,1)}), s8[4194304]{0:T(1024)(128)(4,1)S(1)}, s32[]{:S(2)}) async-start(s8[6291456]{0:T(1024)(128)(4,1)} %bitcast.17), calls=%async_computation.3 | async-start | bytes 8388608
  48.9 20.5 %collective-permute-start.2 = (bf16[384,1024]{1,0:T(8,128)(2,1)}, bf16[384,1024]{1,0:T(8,128)(2,1)}, u32[]{:S(2)}, u32[]{:S(2)}) collective-permute-start(bf16[384,1024]{1,0:T(8,128)(2,1)} %fusion.12), channel_id=1, source_target_pairs={{1,0},{2,1},{3,2},{4,3},{5,4},{6,5},{7,6},{9,8},{10,9},{11,10},{12... | collective-permute-start | bytes 2359304 | tf_op jit(solution)/shard_map/ppermute | solution.py:20
  140.9 2.7 %copy-start.4 = (f32[32,3072]{1,0:T(8,128)S(1)}, f32[32,3072]{1,0:T(8,128)}, u32[]{:S(2)}) copy-start(f32[32,3072]{1,0:T(8,128)} %get-tuple-element.27) | copy-start | bytes 1179652

commit v5 on v4

--- a/solution.py
+++ b/solution.py
@@ -93,9 +93,11 @@
 def reduce_kernel(records, scale, *refs):
     frames, before = refs[:records], refs[records : 2 * records]
     own, earlier = refs[2 * records : 3 * records], refs[3 * records : 4 * records]
-    returned, w_ref = refs[4 * records : 5 * records - 1], refs[5 * records - 1]
+    returned, w_ref = refs[4 * records : 5 * records - 1], refs[-1]
     out_ref, grad_ref, held, landed, sums, leaving, arriving = refs[5 * records : 5 * records + 7]
-    send_sem, recv_sem, back_send_sem, back_recv_sem = refs[5 * records + 7 :]
+    send_sem, recv_sem, back_send_sem, back_recv_sem, load_sem = refs[5 * records + 7 : -1]
+    load = pltpu.make_async_copy(refs[5 * records - 1], w_ref, load_sem)
+    load.start()
     width = frames[0].shape[1]
     streams, blocks = lax.axis_size("stream"), lax.axis_size("tm")
     stream, block = lax.axis_index("stream"), lax.axis_index("tm")
@@ -223,11 +225,12 @@
         else:
             body(0, 0)
 
-    by_columns(returning)
-    pl.when(has_before)(back.start)
     products(1 - dims[first][2])
     for c in range(3):
         copy(c, 0).start()
+    load.wait()
+    by_columns(returning)
+    pl.when(has_before)(back.start)
     products(dims[first][2])
     for phase in range(count):
         if 0 < phase <= records:
@@ -262,7 +265,8 @@
     operands = (*frames, *before, *own, *earlier, *returned, w_qkv)
     return pl.pallas_call(
         functools.partial(reduce_kernel, records, scale),
-        in_specs=[pl.BlockSpec(memory_space=pltpu.VMEM)] * len(operands),
+        in_specs=[pl.BlockSpec(memory_space=pltpu.VMEM)] * (len(operands) - 1)
+        + [pl.BlockSpec(memory_space=pl.ANY)],
         out_specs=[pl.BlockSpec(memory_space=pltpu.VMEM)] * 2,
         out_shape=(
             jax.ShapeDtypeStruct((width // devices, 3 * width), jnp.float32),
@@ -278,6 +282,8 @@
             pltpu.SemaphoreType.DMA((3, count)),
             pltpu.SemaphoreType.DMA,
             pltpu.SemaphoreType.DMA,
+            pltpu.SemaphoreType.DMA,
+            pltpu.VMEM(w_qkv.shape, w_qkv.dtype),
         ],
         compiler_params=pltpu.CompilerParams(collective_id=0, has_side_effects=True),
         cost_estimate=pl.CostEstimate(

time: 145 us -> 149 us (1.028)
  Pallas kernels: 101 us -> 106 us
    pallas_call x1, Pallas kernels: 71.5 us -> 75.7 us  [gradients(): pl.pallas_call(functools.partial(reduce_kernel, records, scale), in_specs...]
  transfers between devices with their start and end apart: 3 -> 3, of which waited for: 1 -> 1; matrix products, arithmetic and copies ran while one was open for 17% -> 16% of each run, Pallas kernels for 21% -> 20%
where the time goes in v5:
time: 149 us
  Pallas kernels  106 us (71%)
  matrix products  23.1 us (16%)
  starting transfers between devices  11.2 us (8%)
  local copies, waits for them, and re-layouts  6.41 us (4%)
  waiting for transfers between devices  1.49 us (1%)
    pallas_call x1, Pallas kernels, gradients(): pl.pallas_call(functools.partial(reduce_kernel, records, scale), in_specs...  75.7 us
    pallas_call x2, Pallas kernels, attention(): pl.pallas_call(functools.partial(attention_kernel, width), grid=(HEADS //...  29.9 us
    dot_general x5, matrix products, dot(): return lax.dot_general(a, b, dims, preferred_element_type=jnp.float32)  23.1 us
    ppermute x3, starting transfers between devices, passed_along(): lax.ppermute(value, axis, [(source, source + steps) for source in range(f...  11.2 us
    unnamed x22, local copies, waits for them, and re-layouts  3.51 us
  transfers between devices with their start and end apart: 3, of which 1 were waited for; matrix products, arithmetic and copies ran while one was open for 16% of the time, Pallas kernels for 20%

profile of v5, /device:TPU:0, one launch (start us, length us, event | category | flops | bytes accessed | tf_op | source)
XLA Modules:
  0.0 148.5 jit_solution(15683839519183732572)
XLA Ops:
  0.6 0.0 copy-start.1
  0.6 0.0 slice-start
  0.7 1.6 %slice_bitcast_fusion.2 = (bf16[384,1024]{1,0:T(8,128)(2,1)S(1)}, bf16[384,1024]{1,0:T(8,128)(2,1)S(1)}) fusion(bf16[2,384,1024]{2,1,0:T(8,128)(2,1)} %param.3), kind=kLoop, calls=%fused_computation.13 | loop fusion | bytes 3145728 | tf_op jit(solution)/shard_map/squeeze | solution.py:314
  2.3 0.0 copy-start.2
  2.3 0.0 copy-start.3
  2.3 5.2 %collective-permute-start = (bf16[384,1024]{1,0:T(8,128)(2,1)S(1)}, bf16[384,1024]{1,0:T(8,128)(2,1)S(1)}, u32[]{:S(2)}, u32[]{:S(2)}) collective-permute-start(bf16[384,1024]{1,0:T(8,128)(2,1)S(1)} %get-tuple-element.23.refs_0_), channel_id=1, source_target_pairs={{0,1},{1,2},{2,3},{3,4},{4,5},{5,6},{6,7},{8,9},{9,10},{10,11},{11... | collective-permute-start | bytes 2359304 | tf_op jit(solution)/shard_map/ppermute | solution.py:20
  7.5 0.0 copy-start
  7.6 0.0 slice-start.1
  7.6 4.5 %collective-permute-start.1 = (bf16[384,1024]{1,0:T(8,128)(2,1)S(1)}, bf16[384,1024]{1,0:T(8,128)(2,1)}, u32[]{:S(2)}, u32[]{:S(2)}) collective-permute-start(bf16[384,1024]{1,0:T(8,128)(2,1)S(1)} %get-tuple-element.22.refs_1_), channel_id=1, source_target_pairs={{0,1},{1,2},{2,3},{3,4},{4,5},{5,6},{6,7},{8,9},{9,10},{10,11},{11... | collective-permute-start | bytes 2359304 | tf_op jit(solution)/shard_map/ppermute | solution.py:20
  12.1 0.0 copy-done.1
  12.1 6.6 %convolution_convert_fusion.1.qkv_ref = bf16[384,3072]{1,0:T(8,128)(2,1)} fusion(bf16[1024,3072]{1,0:T(8,128)(2,1)} %refs_9_.1, bf16[2,384,1024]{2,1,0:T(8,128)(2,1)S(1)} %copy-done.1), kind=kOutput, calls=%fused_computation.1 | convolution fusion | flops 2417098752 | bytes 9437184 | tf_op jit(solution)/shard_map/dot_general | solution.py:24
  18.7 0.0 copy-done.2
  18.7 0.0 copy-done.3
  18.7 0.0 copy-done
  18.7 1.3 slice_bitcast_fusion
  20.0 0.0 slice-done
  20.0 0.0 slice-done.1
  20.0 3.9 %convolution_convert_fusion.qkv_ref = bf16[384,3072]{1,0:T(8,128)(2,1)} fusion(bf16[1024,3072]{1,0:T(8,128)(2,1)S(1)} %bitcast.16, bf16[2,384,1024]{2,1,0:T(8,128)(2,1)S(1)} %copy-done.1), kind=kOutput, calls=%fused_computation | convolution fusion | flops 2417098752 | bytes 9437184 | tf_op jit(solution)/shard_map/dot_general | solution.py:24
  23.9 1.5 collective-permute-done.refs_2_
  25.4 0.0 copy-start.5
  25.4 2.9 %fusion.6.prev_ref = bf16[384,2048]{1,0:T(8,128)(2,1)} fusion(bf16[384,1024]{1,0:T(8,128)(2,1)S(1)} %collective-permute-done.refs_2_, bf16[1024,3072]{1,0:T(8,128)(2,1)S(1)} %bitcast.16), kind=kOutput, calls=%fused_computation.8 | convolution fusion | flops 1611399168 | bytes 6553600 | tf_op jit(solution)/shard_map/dot_general | solution.py:24
  28.3 0.0 copy-done.5
  28.3 0.0 slice-start.2
  28.3 15.0 %shard_map.50 = (bf16[384,3072]{1,0:T(8,128)(2,1)}, bf16[384,2048]{1,0:T(8,128)(2,1)}) custom-call(bf16[384,3072]{1,0:T(8,128)(2,1)} %convolution_convert_fusion.1.qkv_ref, bf16[384,2048]{1,0:T(8,128)(2,1)} %fusion.6.prev_ref, bf16[384,1024]{1,0:T(8,128)(2,1)} %get-tuple-element.21.grad_ref), custom_call_target="tpu_custom_call" | custom-call | flops 3019898880 | bytes 8650752 | tf_op jit(solution)/shard_map/pallas_call | solution.py:75
  43.3 0.0 slice-start.3
  43.3 5.5 %fusion.12 = bf16[384,1024]{1,0:T(8,128)(2,1)} fusion(bf16[384,2048]{1,0:T(8,128)(2,1)} %get-tuple-element.16.refs_6_, bf16[1024,3072]{1,0:T(8,128)(2,1)} %refs_9_.1), kind=kOutput, calls=%fused_computation.10 | convolution fusion | flops 1611005952 | bytes 6553600 | tf_op jit(solution)/shard_map/dot_general | solution.py:24
  48.9 1.5 collective-permute-start.2
  50.3 0.0 collective-permute-done.1.refs_3_
  50.3 0.0 slice-done.2
  50.4 0.0 slice-done.3
  50.4 4.1 %fusion.9.prev_ref = bf16[384,2048]{1,0:T(8,128)(2,1)} fusion(bf16[384,1024]{1,0:T(8,128)(2,1)} %collective-permute-done.1.refs_3_, bf16[1024,3072]{1,0:T(8,128)(2,1)S(1)} %bitcast.18), kind=kOutput, calls=%fused_computation.9 | convolution fusion | flops 1611399168 | bytes 6553600 | tf_op jit(solution)/shard_map/dot_general | solution.py:24
  54.4 14.9 %shard_map.51 = (bf16[384,3072]{1,0:T(8,128)(2,1)}, bf16[384,2048]{1,0:T(8,128)(2,1)}) custom-call(bf16[384,3072]{1,0:T(8,128)(2,1)} %convolution_convert_fusion.qkv_ref, bf16[384,2048]{1,0:T(8,128)(2,1)} %fusion.9.prev_ref, bf16[384,1024]{1,0:T(8,128)(2,1)} %get-tuple-element.20.grad_ref), custom_call_target="tpu_custom_call" | custom-call | flops 3019898880 | bytes 8650752 | tf_op jit(solution)/shard_map/pallas_call | solution.py:75
  69.3 0.0 collective-permute-done.2.refs_8_
  69.3 75.7 %shard_map.52 = (f32[32,3072]{1,0:T(8,128)}, bf16[2,384,1024]{2,1,0:T(8,128)(2,1)}) custom-call(bf16[384,1024]{1,0:T(8,128)(2,1)} %copy-done.3, bf16[384,1024]{1,0:T(8,128)(2,1)} %copy-done.2, bf16[384,1024]{1,0:T(8,128)(2,1)} %copy-done.5, bf16[384,1024]{1,0:T(8,128)(2,1)} %collective-permute-done.1.refs_3_, bf16[384,3072]{1,0:T(8,128)(2,1)} %get-tuple-element.13.refs_4_, ...), custom_call_target="tpu_custom_call" | custom-call | flops 16106127360 | bytes 17301504 | tf_op jit(solution)/shard_map/pallas_call | solution.py:266
  145.0 0.0 copy-start.4
  145.0 2.7 %copy.7 = bf16[2,384,1024]{2,1,0:T(8,128)(2,1)} copy(bf16[2,384,1024]{2,1,0:T(8,128)(2,1)} %get-tuple-element.26) | data formatting | bytes 3145728
  147.8 0.0 copy-done.4
  147.8 0.7 copy.8
  (2 shorter events, 0.0 us)
Async XLA Ops:
  0.6 11.5 %copy-start.1 = (bf16[2,384,1024]{2,1,0:T(8,128)(2,1)S(1)}, bf16[2,384,1024]{2,1,0:T(8,128)(2,1)}, u32[]{:S(2)}) copy-start(bf16[2,384,1024]{2,1,0:T(8,128)(2,1)} %param.3) | copy-start | bytes 4718596
  0.6 19.4 %slice-start = ((s8[6291456]{0:T(1024)(128)(4,1)}), s8[4194304]{0:T(1024)(128)(4,1)S(1)}, s32[]{:S(2)}) async-start(s8[6291456]{0:T(1024)(128)(4,1)} %bitcast.15), calls=%async_computation | async-start | bytes 8388608
  2.3 16.4 %copy-start.2 = (bf16[384,1024]{1,0:T(8,128)(2,1)}, bf16[384,1024]{1,0:T(8,128)(2,1)S(1)}, u32[]{:S(2)}) copy-start(bf16[384,1024]{1,0:T(8,128)(2,1)S(1)} %get-tuple-element.22.refs_1_) | copy-start | bytes 2359300
  2.3 16.4 %copy-start.3 = (bf16[384,1024]{1,0:T(8,128)(2,1)}, bf16[384,1024]{1,0:T(8,128)(2,1)S(1)}, u32[]{:S(2)}) copy-start(bf16[384,1024]{1,0:T(8,128)(2,1)S(1)} %get-tuple-element.23.refs_0_) | copy-start | bytes 2359300
  2.3 23.1 %collective-permute-start = (bf16[384,1024]{1,0:T(8,128)(2,1)S(1)}, bf16[384,1024]{1,0:T(8,128)(2,1)S(1)}, u32[]{:S(2)}, u32[]{:S(2)}) collective-permute-start(bf16[384,1024]{1,0:T(8,128)(2,1)S(1)} %get-tuple-element.23.refs_0_), channel_id=1, source_target_pairs={{0,1},{1,2},{2,3},{3,4},{4,5},{5,6},{6,7},{8,9},{9,10},{10,11},{11... | collective-permute-start | bytes 2359304 | tf_op jit(solution)/shard_map/ppermute | solution.py:20
  7.5 11.2 %copy-start = (bf16[2,384,1024]{2,1,0:T(8,128)(2,1)S(1)}, bf16[2,384,1024]{2,1,0:T(8,128)(2,1)}, u32[]{:S(2)}) copy-start(bf16[2,384,1024]{2,1,0:T(8,128)(2,1)} %param.5) | copy-start | bytes 4718596
  7.6 12.4 %slice-start.1 = ((s8[6291456]{0:T(1024)(128)(4,1)}), s8[2097152]{0:T(1024)(128)(4,1)S(1)}, s32[]{:S(2)}) async-start(s8[6291456]{0:T(1024)(128)(4,1)} %bitcast.15), calls=%async_computation.1 | async-start | bytes 4194304
  7.6 42.8 %collective-permute-start.1 = (bf16[384,1024]{1,0:T(8,128)(2,1)S(1)}, bf16[384,1024]{1,0:T(8,128)(2,1)}, u32[]{:S(2)}, u32[]{:S(2)}) collective-permute-start(bf16[384,1024]{1,0:T(8,128)(2,1)S(1)} %get-tuple-element.22.refs_1_), channel_id=1, source_target_pairs={{0,1},{1,2},{2,3},{3,4},{4,5},{5,6},{6,7},{8,9},{9,10},{10,11},{11... | collective-permute-start | bytes 2359304 | tf_op jit(solution)/shard_map/ppermute | solution.py:20
  25.4 2.9 %copy-start.5 = (bf16[384,1024]{1,0:T(8,128)(2,1)}, bf16[384,1024]{1,0:T(8,128)(2,1)S(1)}, u32[]{:S(2)}) copy-start(bf16[384,1024]{1,0:T(8,128)(2,1)S(1)} %collective-permute-done.refs_2_) | copy-start | bytes 2359300
  28.3 22.0 %slice-start.2 = ((s8[6291456]{0:T(1024)(128)(4,1)}), s8[2097152]{0:T(1024)(128)(4,1)S(1)}, s32[]{:S(2)}) async-start(s8[6291456]{0:T(1024)(128)(4,1)} %bitcast.17), calls=%async_computation.2 | async-start | bytes 4194304
  43.3 7.0 %slice-start.3 = ((s8[6291456]{0:T(1024)(128)(4,1)}), s8[4194304]{0:T(1024)(128)(4,1)S(1)}, s32[]{:S(2)}) async-start(s8[6291456]{0:T(1024)(128)(4,1)} %bitcast.17), calls=%async_computation.3 | async-start | bytes 8388608
  48.9 20.5 %collective-permute-start.2 = (bf16[384,1024]{1,0:T(8,128)(2,1)}, bf16[384,1024]{1,0:T(8,128)(2,1)}, u32[]{:S(2)}, u32[]{:S(2)}) collective-permute-start(bf16[384,1024]{1,0:T(8,128)(2,1)} %fusion.12), channel_id=1, source_target_pairs={{1,0},{2,1},{3,2},{4,3},{5,4},{6,5},{7,6},{9,8},{10,9},{11,10},{12... | collective-permute-start | bytes 2359304 | tf_op jit(solution)/shard_map/ppermute | solution.py:20
  145.0 2.7 %copy-start.4 = (f32[32,3072]{1,0:T(8,128)S(1)}, f32[32,3072]{1,0:T(8,128)}, u32[]{:S(2)}) copy-start(f32[32,3072]{1,0:T(8,128)} %get-tuple-element.27) | copy-start | bytes 1179652
